TPU v7x, 512 devices: a whole 4x4x16 slice. The times are simulated.
512 devices in a mesh: section: 8 (over y_lo, x), tp: 16 (over z), dp: 4 (over y_hi, core).
Axes of the slice: x: 4, y: 4 (y_hi: 2, y_lo: 2; y = y_hi * 2 + y_lo), z: 16, core: 2. Of those that a mesh axis runs over, the one named last changes fastest.
Arguments:
- stream: bfloat16 [8, 16, 32, 4096], P('section', 'dp', None, 'tp'), may hold values from -120 to 120
- memory_hidden: bfloat16 [16, 32, 4096], P('dp', 'section', 'tp'), may hold values from -120 to 120
- layer_gain: float32 [8, 4096], P('section'), may hold values from 0.5 to 4
- final_gain: float32 [4096], replicated, may hold values from 0.5 to 4
- query_weight: bfloat16 [8, 4096, 4096], P('section', 'dp', 'tp'), may hold values from -0.09375 to 0.09375
- key_weight: bfloat16 [8, 4096, 4096], P('section', 'dp', 'tp'), may hold values from -0.09375 to 0.09375
- value_weight: bfloat16 [8, 4096, 4096], P('section', 'dp', 'tp'), may hold values from -0.09375 to 0.09375
- cotangent: bfloat16 [8, 16, 32, 4096], P('section', 'dp', None, 'tp'), may hold values from -6 to 6
- encoder_lengths: int32 [16], P('dp'), may hold values from 8 to 32
- decoder_lengths: int32 [16], P('dp'), may hold values from 8 to 32
- assignment: int32 [4, 4], P('dp'), may hold values from 0 to 3, each once within a row
Outputs:
- attention_mix: bfloat16 [8, 16, 32, 4096], P('section', 'dp', None, 'tp')
- stream_grad: bfloat16 [8, 16, 32, 4096], P('section', 'dp', None, 'tp')
- memory_grad: bfloat16 [16, 32, 4096], P('dp', 'section', 'tp')
- query_weight_grad: bfloat16 [8, 4096, 4096], P('section', 'dp', 'tp')
- key_weight_grad: bfloat16 [8, 4096, 4096], P('section', 'dp', 'tp')
- value_weight_grad: bfloat16 [8, 4096, 4096], P('section', 'dp', 'tp')
Inputs may be any that keep to these rules, and one draw needn't show every extreme that they name: Each row of assignment is a permutation of 0 to 3.
All inputs are finite; a program needn't handle non-finite values.
Results may differ from a plain program's by a relative error of at most 0.019.
The roundings to bfloat16 on the way count: a program that leaves them out, or rounds other values in their place, can miss the bound.
Values may be sent and summed in bfloat16 or wider, within the bound.
A program may use at most 64 MiB of HBM per device.

v0:
```python
import jax
import jax.numpy as jnp
from jax import lax
from jax.sharding import PartitionSpec as P

HEAD_DIM = 64


EPSILON = 1e-06


def sent_to_all(array, axis):
    copies = jnp.broadcast_to(array, (lax.axis_size(axis), *array.shape))
    return lax.all_to_all(copies, axis, split_axis=0, concat_axis=0, tiled=True)


def in_order(pieces, dim):
    pieces = jnp.moveaxis(pieces, 0, dim)
    shape = pieces.shape
    return pieces.reshape(*shape[:dim], shape[dim] * shape[dim + 1], *shape[dim + 2 :])


def gather_directly(array, axis, dim):
    pieces = sent_to_all(array, axis)
    return in_order(pieces, dim)


def sent_together(arrays, axis, dim, along):
    widths = [a.shape[along] for a in arrays]
    both = jnp.concatenate(arrays, axis=along)
    out = lax.all_gather(both, axis, axis=dim, tiled=True)
    return tuple(jnp.split(out, [sum(widths[:k]) for k in range(1, len(widths))], axis=along))


def of_everyone(array, axis):
    everything = sent_to_all(array, axis)
    return jnp.sum(everything, axis=0)


def in_blocks(array, dim, count):
    shape = array.shape
    pieces = array.reshape(*shape[:dim], count, shape[dim] // count, *shape[dim + 1 :])
    return jnp.moveaxis(pieces, dim, 0)


def summed_on_arrival(array, axis, dim):
    pieces = in_blocks(array, dim, lax.axis_size(axis))
    arrived = lax.all_to_all(pieces, axis, split_axis=0, concat_axis=0, tiled=True)
    return arrived.sum(axis=0)


def side_by_side(arrays, axis, split_dim, concat_dim, along):
    widths = [a.shape[along] for a in arrays]
    both = jnp.concatenate(arrays, axis=along)
    out = lax.all_to_all(both, axis, split_axis=split_dim, concat_axis=concat_dim, tiled=True)
    return tuple(jnp.split(out, [sum(widths[:k]) for k in range(1, len(widths))], axis=along))


def normalize(hidden_in, gain):
    floats = hidden_in.astype(jnp.float32)
    inverse = lax.rsqrt(jnp.mean(floats * floats, axis=-1, keepdims=True) + EPSILON)
    return (floats, inverse, (floats * inverse * gain).astype(jnp.bfloat16))


def contract_last(left, right):
    return lax.dot_general(
        left, right, (((1,), (1,)), ((), ())), preferred_element_type=jnp.float32
    )


def contract_rows(left, right):
    return lax.dot_general(
        left, right, (((0, 1), (0, 1)), ((), ())), preferred_element_type=jnp.float32
    )


def attention_core(queries, keys, values, raw_upstream, query_len, key_len):
    span = queries.shape[1]
    score_scale = queries.shape[3] ** (-0.5)
    positions = jnp.arange(span, dtype=jnp.int32)
    key_live = positions[None, :] < key_len[:, None]
    row_live = (positions[None, :] < query_len[:, None]).astype(jnp.float32)[:, :, None, None]
    scores = (
        jnp.einsum("bqhe,bkhe->bhqk", queries, keys, preferred_element_type=jnp.float32)
        * score_scale
    )
    scores = jnp.where(key_live[:, None, None, :], scores, -1e30)
    weights = jax.nn.softmax(scores, axis=-1)
    probs = weights.astype(jnp.bfloat16)
    mixture = (
        jnp.einsum("bhqk,bkhe->bqhe", probs, values, preferred_element_type=jnp.float32) * row_live
    ).astype(jnp.bfloat16)
    upstream = (raw_upstream.astype(jnp.float32) * row_live).astype(jnp.bfloat16)
    grad_values = jnp.einsum(
        "bhqk,bqhe->bkhe", probs, upstream, preferred_element_type=jnp.float32
    ).astype(jnp.bfloat16)
    grad_weights = jnp.einsum(
        "bqhe,bkhe->bhqk", upstream, values, preferred_element_type=jnp.float32
    )
    grad_scores = (
        weights
        * (grad_weights - jnp.sum(grad_weights * weights, axis=-1, keepdims=True))
        * score_scale
    ).astype(jnp.bfloat16)
    grad_queries = jnp.einsum(
        "bhqk,bkhe->bqhe", grad_scores, keys, preferred_element_type=jnp.float32
    ).astype(jnp.bfloat16)
    grad_keys = jnp.einsum(
        "bhqk,bqhe->bkhe", grad_scores, queries, preferred_element_type=jnp.float32
    ).astype(jnp.bfloat16)
    return (mixture, grad_queries, grad_keys, grad_values)


def shards(
    stream,
    memory_hidden,
    layer_gain,
    final_gain,
    query_weight,
    key_weight,
    value_weight,
    cotangent,
    encoder_lengths,
    decoder_lengths,
    assignment,
):
    section_index = lax.axis_index("section")
    decoder = section_index >= lax.axis_size("section") // 2
    group_index = lax.axis_index("tp")
    local_rows = stream[0]
    micro_count, span_length, share_width = local_rows.shape
    hidden = share_width * lax.axis_size("tp")
    columns = query_weight.shape[2]
    token_count = micro_count * span_length
    layer_share = lax.dynamic_slice_in_dim(layer_gain[0], group_index * share_width, share_width)
    final_share = lax.dynamic_slice_in_dim(final_gain, group_index * share_width, share_width)
    gathered = gather_directly(local_rows, "tp", 2)
    floats, inverse, normed = normalize(gathered, layer_gain[0])
    memory_rows = gather_directly(memory_hidden, "section", 1)
    memory_full = gather_directly(memory_rows, "tp", 2)
    unused, memory_inverse, memory = normalize(memory_full, final_gain)
    selector = assignment[0][:, None] == jnp.arange(micro_count, dtype=jnp.int32)[None, :]
    memory_chosen = jnp.einsum(
        "mn,nsd->msd", selector.astype(jnp.bfloat16), memory, preferred_element_type=jnp.float32
    ).astype(jnp.bfloat16)
    decoder_keys = jnp.sum(jnp.where(selector, encoder_lengths[None, :], 0), axis=1)
    source = jnp.where(decoder, memory_chosen, normed)
    query_len = jnp.where(decoder, decoder_lengths, encoder_lengths)
    key_len = jnp.where(decoder, decoder_keys, encoder_lengths)
    flat_normed = normed.reshape(token_count, hidden)
    flat_source = source.reshape(token_count, hidden)
    full_query, full_key, full_value = sent_together(
        (query_weight[0], key_weight[0], value_weight[0]), "dp", 0, 1
    )
    queries = jnp.dot(flat_normed, full_query, preferred_element_type=jnp.float32).astype(
        jnp.bfloat16
    )
    keys = jnp.dot(flat_source, full_key, preferred_element_type=jnp.float32).astype(jnp.bfloat16)
    values = jnp.dot(flat_source, full_value, preferred_element_type=jnp.float32).astype(
        jnp.bfloat16
    )
    heads_here = columns // HEAD_DIM
    four_dims = (micro_count, span_length, heads_here, HEAD_DIM)
    mixture, grad_queries, grad_keys, grad_values = attention_core(
        queries.reshape(four_dims),
        keys.reshape(four_dims),
        values.reshape(four_dims),
        cotangent[0].reshape(four_dims),
        query_len,
        key_len,
    )
    flat_grad_queries = grad_queries.reshape(token_count, columns)
    flat_grad_keys = grad_keys.reshape(token_count, columns)
    flat_grad_values = grad_values.reshape(token_count, columns)
    back_query = contract_last(flat_grad_queries, full_query)
    back_source = contract_last(flat_grad_keys, full_key) + contract_last(
        flat_grad_values, full_value
    )
    normed_part = (back_query + jnp.where(decoder, 0.0, back_source)).reshape(
        micro_count, span_length, hidden
    )
    memory_part = jnp.where(decoder, back_source, 0.0).reshape(micro_count, span_length, hidden)
    grad_share = lax.psum_scatter(
        normed_part.astype(jnp.bfloat16), "tp", scatter_dimension=2, tiled=True
    ).astype(jnp.float32)
    input_share = local_rows.astype(jnp.float32)
    products = of_everyone(
        jnp.sum(input_share * layer_share * grad_share, axis=-1, keepdims=True), "tp"
    )
    stream_out = inverse * (
        layer_share * grad_share - input_share * (inverse * inverse) * (products / hidden)
    )
    per_sample = jnp.einsum(
        "mn,msd->nsd", selector.astype(jnp.float32), memory_part, precision=lax.Precision.HIGHEST
    )
    by_tokens = summed_on_arrival(per_sample, "section", 1)
    by_share = summed_on_arrival(by_tokens, "tp", 2)
    rows_here = by_share.shape[1]
    inverse_here = lax.dynamic_slice_in_dim(memory_inverse, section_index * rows_here, rows_here, 1)
    memory_floats = memory_hidden.astype(jnp.float32)
    memory_products = of_everyone(
        jnp.sum(memory_floats * final_share * by_share, axis=-1, keepdims=True), "tp"
    )
    memory_out = inverse_here * (
        final_share * by_share
        - memory_floats * (inverse_here * inverse_here) * (memory_products / hidden)
    )
    moved_normed, moved_source = side_by_side((normed, source), "dp", 2, 0, 1)
    pieces = sent_together(
        (
            grad_queries.reshape(micro_count, span_length, columns),
            grad_keys.reshape(micro_count, span_length, columns),
            grad_values.reshape(micro_count, span_length, columns),
        ),
        "dp",
        0,
        1,
    )
    return (
        mixture.reshape(micro_count, span_length, columns)[None],
        stream_out.astype(jnp.bfloat16)[None],
        memory_out.astype(jnp.bfloat16),
        contract_rows(moved_normed, pieces[0]).astype(jnp.bfloat16)[None],
        contract_rows(moved_source, pieces[1]).astype(jnp.bfloat16)[None],
        contract_rows(moved_source, pieces[2]).astype(jnp.bfloat16)[None],
    )


def solution(mesh):
    placed = (
        P("section", "dp", None, "tp"),
        P("dp", "section", "tp"),
        P("section", None),
        P(),
        P("section", "dp", "tp"),
        P("section", "dp", "tp"),
        P("section", "dp", "tp"),
        P("section", "dp", None, "tp"),
        P("dp"),
        P("dp"),
        P("dp", None),
    )
    return jax.shard_map(
        shards,
        mesh=mesh,
        in_specs=placed,
        out_specs=(
            P("section", "dp", None, "tp"),
            P("section", "dp", None, "tp"),
            P("dp", "section", "tp"),
            P("section", "dp", "tp"),
            P("section", "dp", "tp"),
            P("section", "dp", "tp"),
        ),
        check_vma=False,
    )
```

profile of v0, /device:TPU:6, one launch (start us, length us, event | category | flops | bytes accessed | tf_op | source)
XLA Modules:
  0.0 331.8 jit_solution(16533793122381087119)
XLA Ops:
  8.0 12.6 %all_to_all.53 = bf16[8,4,4,256]{3,1,2,0:T(4,128)(2,1)S(1)} all-to-all(bf16[8,4,4,256]{3,1,2,0:T(4,128)(2,1)S(1)} %broadcast_in_dim.48), channel_id=1, replica_groups=mesh['section'=8,'tp'=16,'dp'=4] {'section'}, dimensions={0} | all-to-all | bytes 131072 | tf_op jit(solution)/shard_map/all_to_all | solution.py:14
  22.6 12.6 %all-to-all-start.2 = ((bf16[16,4,32,256]{3,2,1,0:T(8,128)(2,1)}), bf16[16,4,32,256]{3,2,1,0:T(8,128)(2,1)S(1)}, u32[]{:S(2)}, u32[]{:S(2)}) async-start(bf16[16,4,32,256]{3,2,1,0:T(8,128)(2,1)} %broadcast_in_dim.79), calls=%async_computation.2 | async-start | bytes 2097152 | tf_op jit(solution)/shard_map/all_to_all | solution.py:14
  36.6 46.3 %all-to-all-done.2 = bf16[16,4,32,256]{3,2,1,0:T(8,128)(2,1)S(1)} async-done(((bf16[16,4,32,256]{3,2,1,0:T(8,128)(2,1)}), bf16[16,4,32,256]{3,2,1,0:T(8,128)(2,1)S(1)}, u32[]{:S(2)}, u32[]{:S(2)}) %all-to-all-start.2) | async-done | bytes 1048608 | tf_op jit(solution)/shard_map/all_to_all | solution.py:14
  84.3 8.7 %all-to-all-start.1 = ((bf16[16,4,32,256]{3,1,2,0:T(4,128)(2,1)}), bf16[16,4,32,256]{3,1,2,0:T(4,128)(2,1)S(1)}, u32[]{:S(2)}, u32[]{:S(2)}) async-start(bf16[16,4,32,256]{3,1,2,0:T(4,128)(2,1)} %broadcast_in_dim.78), calls=%async_computation.1 | async-start | bytes 2097152 | tf_op jit(solution)/shard_map/all_to_all | solution.py:14
  94.2 2.6 copy.167
  96.8 2.6 copy.170
  100.9 3.2 reshape.186
  104.2 4.7 %copy.197 = f32[16,8,16,256]{3,1,2,0:T(8,128)} copy(f32[16,8,16,256]{3,2,1,0:T(8,128)} %bitcast.101) | data formatting | bytes 4194304
  109.5 33.4 %all-to-all-done.1 = bf16[16,4,32,256]{3,1,2,0:T(4,128)(2,1)S(1)} async-done(((bf16[16,4,32,256]{3,1,2,0:T(4,128)(2,1)}), bf16[16,4,32,256]{3,1,2,0:T(4,128)(2,1)S(1)}, u32[]{:S(2)}, u32[]{:S(2)}) %all-to-all-start.1) | async-done | bytes 1048608 | tf_op jit(solution)/shard_map/all_to_all | solution.py:14
  143.2 2.6 copy.162
  145.8 2.8 reshape.185
  155.7 5.1 %copy.186 = bf16[4,64,4096]{1,0,2:T(4,128)(2,1)} copy(bf16[4,64,4096]{2,0,1:T(4,128)(2,1)S(1)} %pad_maximum_fusion) | data formatting | bytes 4194304 | tf_op jit(solution)/shard_map/concatenate | solution.py:54
  160.8 5.9 %reshape.196 = bf16[4,2,131072]{2,1,0:T(2,128)(2,1)} reshape(bf16[4096,4,64]{2,1,0:T(4,128)(2,1)} %bitcast.98) | data formatting | bytes 4194304
  166.7 4.2 %all-to-all-start.7 = ((bf16[4,2,131072]{2,1,0:T(2,128)(2,1)}), bf16[4,2,131072]{2,1,0:T(2,128)(2,1)S(1)}, u32[]{:S(2)}, u32[]{:S(2)}) async-start(bf16[4,2,131072]{2,1,0:T(2,128)(2,1)} %reshape.196), calls=%async_computation.8 | async-start | bytes 4194304 | tf_op jit(solution)/shard_map/all_to_all | solution.py:55
  170.9 2.7 fusion.34
  174.6 2.7 fusion.40
  178.3 2.8 fusion.37
  187.2 3.8 %broadcast_select_fusion = (f32[128,4096]{1,0:T(8,128)}, f32[128,4096]{1,0:T(8,128)S(1)}) fusion(pred[]{:T(512)S(6)} %ge.3, f32[128,4096]{1,0:T(8,128)S(1)} %fusion.6, bf16[128,256]{1,0:T(8,128)(2,1)S(1)} %reshape.179, bf16[4096,768]{1,0:T(8,128)(2,1)} %all-gather.2.cloned.1.call-done), kind=kOutput, calls=%fused_computation.60 | convolution fusion | flops 269484032 | bytes 8454145 | tf_op jit(solution)/shard_map/dot_general | solution.py:66
  191.0 3.5 %fusion.2 = bf16[128,4096]{1,0:T(8,128)(2,1)} fusion(bf16[128,256]{1,0:T(8,128)(2,1)S(1)} %reshape.177, f32[128,4096]{1,0:T(8,128)S(1)} %get-tuple-element.15, bf16[4096,768]{1,0:T(8,128)(2,1)} %all-gather.2.cloned.1.call-done, pred[]{:T(512)S(6)} %ge.3), kind=kOutput, calls=%fused_computation.5 | convolution fusion | flops 270008320 | bytes 5308417 | tf_op jit(solution)/shard_map/dot_general | solution.py:66
  194.5 2.9 copy.184
  197.5 3.5 %convolution_bitcast_fusion = f32[8,4,4,4096]{3,1,2,0:T(4,128)} fusion(f32[8,4,4096,4]{2,3,1,0:T(4,128)S(1)} %bitcast.102, s32[4]{0:T(128)S(1)} %bitcast.121), kind=kOutput, calls=%fused_computation.2 | convolution fusion | flops 25165840 | bytes 4194320 | tf_op jit(solution)/shard_map/mn,msd->nsd/dot_general | solution.py:193
  200.9 6.4 %all-to-all-start.4 = ((f32[8,4,4,4096]{3,1,2,0:T(4,128)}), f32[8,4,4,4096]{3,1,2,0:T(4,128)}, u32[]{:S(2)}, u32[]{:S(2)}) async-start(f32[8,4,4,4096]{3,1,2,0:T(4,128)} %convolution_bitcast_fusion), calls=%async_computation.5 | async-start | bytes 4194304 | tf_op jit(solution)/shard_map/all_to_all | solution.py:48
  208.1 4.0 %reshape.197 = bf16[4096,4,64]{2,1,0:T(4,128)(2,1)} reshape(bf16[4,2,131072]{2,1,0:T(2,128)(2,1)S(1)} %all-to-all-done.7) | data formatting | bytes 4194304
  212.1 5.6 %copy.187 = bf16[4,64,4,1024]{3,1,0,2:T(8,128)(2,1)S(1)} copy(bf16[4,64,4,1024]{1,0,3,2:T(4,128)(2,1)} %bitcast.99) | data formatting | bytes 4194304 | tf_op jit(solution)/shard_map/all_to_all | solution.py:55
  218.2 21.7 %all_gather.7 = bf16[16,96,256]{2,1,0:T(8,128)(2,1)S(1)} all-gather(bf16[4,96,256]{2,1,0:T(8,128)(2,1)S(1)} %pad_maximum_fusion.2), channel_id=1, replica_groups=mesh['section'=8,'tp'=16,'dp'=4] {'dp'}, dimensions={0}, use_global_device_ids=true | all-gather | bytes 983040 | tf_op jit(solution)/shard_map/all_gather | solution.py:31
  241.3 21.8 %reduce-scatter.2.cloned.1.call-done = bf16[4,32,256]{2,1,0:T(8,128)(2,1)} async-done(((bf16[4,32,4096]{2,1,0:T(8,128)(2,1)}), bf16[4,32,256]{2,1,0:T(8,128)(2,1)}) %reduce-scatter.2.cloned.1.call-update) | async-done | bytes 65552 | tf_op jit(solution)/shard_map/reduce_scatter | solution.py:183
  264.7 8.8 %all-to-all-start.3 = ((f32[16,1,128]{2,1,0:T(1,128)}), f32[16,1,128]{2,1,0:T(1,128)S(1)}, u32[]{:S(2)}, u32[]{:S(2)}) async-start(f32[16,1,128]{2,1,0:T(1,128)} %reshape.194), calls=%async_computation.4 | async-start | bytes 16384 | tf_op jit(solution)/shard_map/all_to_all | solution.py:14
  278.8 7.2 %all-to-all-done.3 = f32[16,1,128]{2,1,0:T(1,128)S(1)} async-done(((f32[16,1,128]{2,1,0:T(1,128)}), f32[16,1,128]{2,1,0:T(1,128)S(1)}, u32[]{:S(2)}, u32[]{:S(2)}) %all-to-all-start.3) | async-done | bytes 8224 | tf_op jit(solution)/shard_map/all_to_all | solution.py:14
  286.0 4.8 %all-to-all-start.5 = ((f32[16,4,4,256]{3,2,1,0:T(4,128)}), f32[16,4,4,256]{3,2,1,0:T(4,128)S(1)}, u32[]{:S(2)}, u32[]{:S(2)}) async-start(f32[16,4,4,256]{3,2,1,0:T(4,128)} %bitcast.97), calls=%async_computation.6 | async-start | bytes 524288 | tf_op jit(solution)/shard_map/all_to_all | solution.py:48
  294.8 9.9 %all-to-all-done.5 = f32[16,4,4,256]{3,2,1,0:T(4,128)S(1)} async-done(((f32[16,4,4,256]{3,2,1,0:T(4,128)}), f32[16,4,4,256]{3,2,1,0:T(4,128)S(1)}, u32[]{:S(2)}, u32[]{:S(2)}) %all-to-all-start.5) | async-done | bytes 262176 | tf_op jit(solution)/shard_map/all_to_all | solution.py:48
  305.4 6.2 %all-to-all-start.6 = ((f32[16,4,4,1]{2,1,3,0:T(4,128)}), f32[16,4,4,1]{2,1,3,0:T(4,128)S(1)}, u32[]{:S(2)}, u32[]{:S(2)}) async-start(f32[16,4,4,1]{2,1,3,0:T(4,128)} %broadcast_in_dim.87), calls=%async_computation.7 | async-start | bytes 65536 | tf_op jit(solution)/shard_map/all_to_all | solution.py:14
  312.4 11.8 %all-to-all-done.6 = f32[16,4,4,1]{2,1,3,0:T(4,128)S(1)} async-done(((f32[16,4,4,1]{2,1,3,0:T(4,128)}), f32[16,4,4,1]{2,1,3,0:T(4,128)S(1)}, u32[]{:S(2)}, u32[]{:S(2)}) %all-to-all-start.6) | async-done | bytes 1056 | tf_op jit(solution)/shard_map/all_to_all | solution.py:14
  (140 shorter events, 39.8 us)
Async XLA Ops:
  7.2 28.0 %copy-start.5 = (bf16[1,1024,256]{2,1,0:T(8,128)(2,1)S(1)}, bf16[1,1024,256]{2,1,0:T(8,128)(2,1)}, u32[]{:S(2)}) copy-start(bf16[1,1024,256]{2,1,0:T(8,128)(2,1)} %param.17) | copy-start | bytes 1572868
  7.2 28.0 %copy-start.6 = (bf16[1,1024,256]{2,1,0:T(8,128)(2,1)S(1)}, bf16[1,1024,256]{2,1,0:T(8,128)(2,1)}, u32[]{:S(2)}) copy-start(bf16[1,1024,256]{2,1,0:T(8,128)(2,1)} %param.16) | copy-start | bytes 1572868
  7.2 28.0 %copy-start.7 = (bf16[1,1024,256]{2,1,0:T(8,128)(2,1)S(1)}, bf16[1,1024,256]{2,1,0:T(8,128)(2,1)}, u32[]{:S(2)}) copy-start(bf16[1,1024,256]{2,1,0:T(8,128)(2,1)} %param.15) | copy-start | bytes 1572868
  22.6 60.3 %all-to-all-start.2 = ((bf16[16,4,32,256]{3,2,1,0:T(8,128)(2,1)}), bf16[16,4,32,256]{3,2,1,0:T(8,128)(2,1)S(1)}, u32[]{:S(2)}, u32[]{:S(2)}) async-start(bf16[16,4,32,256]{3,2,1,0:T(8,128)(2,1)} %broadcast_in_dim.79), calls=%async_computation.2 | async-start | bytes 2097152 | tf_op jit(solution)/shard_map/all_to_all | solution.py:14
  35.2 135.8 %all-gather.2.cloned.1.call-start = ((), (), s32[]{:S(2)}) async-start(), calls=%async_computation.9 | async-start | bytes 7864320 | tf_op jit(solution)/shard_map/all_gather | solution.py:31
  36.5 56.5 %copy-start.14 = (bf16[1,4,32,256]{3,2,1,0:T(8,128)(2,1)S(1)}, bf16[1,4,32,256]{3,2,1,0:T(8,128)(2,1)}, u32[]{:S(2)}) copy-start(bf16[1,4,32,256]{3,2,1,0:T(8,128)(2,1)} %param.18) | copy-start | bytes 196612
  36.5 56.6 %copy-start.23 = (s32[1,4]{1,0:T(1,128)S(1)}, s32[1,4]{1,0:T(1,128)}, u32[]{:S(2)}) copy-start(s32[1,4]{1,0:T(1,128)} %param.21) | copy-start | bytes 52
  36.5 56.6 %copy-start.27 = (s32[4]{0:T(128)S(1)}, s32[4]{0:T(128)}, u32[]{:S(2)}) copy-start(s32[4]{0:T(128)} %param.19) | copy-start | bytes 52
  36.5 56.7 %copy-start.28 = (s32[4]{0:T(128)S(1)}, s32[4]{0:T(128)}, u32[]{:S(2)}) copy-start(s32[4]{0:T(128)} %param.20) | copy-start | bytes 52
  84.3 58.6 %all-to-all-start.1 = ((bf16[16,4,32,256]{3,1,2,0:T(4,128)(2,1)}), bf16[16,4,32,256]{3,1,2,0:T(4,128)(2,1)S(1)}, u32[]{:S(2)}, u32[]{:S(2)}) async-start(bf16[16,4,32,256]{3,1,2,0:T(4,128)(2,1)} %broadcast_in_dim.78), calls=%async_computation.1 | async-start | bytes 2097152 | tf_op jit(solution)/shard_map/all_to_all | solution.py:14
  104.2 4.7 %copy-start = (f32[4,32,4096]{2,0,1:T(4,128)S(1)}, f32[4,32,4096]{2,0,1:T(4,128)}, u32[]{:S(2)}) copy-start(f32[4,32,4096]{2,0,1:T(4,128)} %reshape.186) | copy-start | bytes 6291460
  104.2 4.7 %copy-start.13 = (f32[1,4096]{1,0:T(1,128)S(1)}, f32[1,4096]{1,0:T(1,128)}, u32[]{:S(2)}) copy-start(f32[1,4096]{1,0:T(1,128)} %param.13) | copy-start | bytes 49156
  166.7 4.2 %copy-start.1 = (bf16[4,32,4096]{2,1,0:T(8,128)(2,1)S(1)}, bf16[4,32,4096]{2,1,0:T(8,128)(2,1)}, u32[]{:S(2)}) copy-start(bf16[4,32,4096]{2,1,0:T(8,128)(2,1)} %copy.169) | copy-start | bytes 3145732
  166.7 34.3 %all-to-all-start.7 = ((bf16[4,2,131072]{2,1,0:T(2,128)(2,1)}), bf16[4,2,131072]{2,1,0:T(2,128)(2,1)S(1)}, u32[]{:S(2)}, u32[]{:S(2)}) async-start(bf16[4,2,131072]{2,1,0:T(2,128)(2,1)} %reshape.196), calls=%async_computation.8 | async-start | bytes 4194304 | tf_op jit(solution)/shard_map/all_to_all | solution.py:55
  170.9 92.2 %reduce-scatter.2.cloned.1.call-start = ((), (), s32[]{:S(2)}) async-start(), calls=%async_computation.10 | async-start | bytes 1114112 | tf_op jit(solution)/shard_map/reduce_scatter | solution.py:183
  174.6 6.9 %copy-start.3 = (bf16[4,32,4,64]{3,2,1,0:T(4,128)(2,1)}, bf16[4,32,4,64]{3,2,1,0:T(4,128)(2,1)S(1)}, u32[]{:S(2)}) copy-start(bf16[4,32,4,64]{3,2,1,0:T(4,128)(2,1)S(1)} %reshape.174) | copy-start | bytes 196612
  178.3 5.5 %copy-start.9 = (bf16[4,32,4,64]{3,2,1,0:T(4,128)(2,1)}, bf16[4,32,4,64]{3,2,1,0:T(4,128)(2,1)S(1)}, u32[]{:S(2)}) copy-start(bf16[4,32,4,64]{3,2,1,0:T(4,128)(2,1)S(1)} %reshape.176) | copy-start | bytes 196612
  200.9 7.1 %copy-start.19 = (f32[4,32]{1,0:T(4,128)S(1)}, f32[4,32]{1,0:T(4,128)}, u32[]{:S(2)}) copy-start(f32[4,32]{1,0:T(4,128)} %copy-done.18) | copy-start | bytes 1540
  200.9 63.8 %all-to-all-start.4 = ((f32[8,4,4,4096]{3,1,2,0:T(4,128)}), f32[8,4,4,4096]{3,1,2,0:T(4,128)}, u32[]{:S(2)}, u32[]{:S(2)}) async-start(f32[8,4,4,4096]{3,1,2,0:T(4,128)} %convolution_bitcast_fusion), calls=%async_computation.5 | async-start | bytes 4194304 | tf_op jit(solution)/shard_map/all_to_all | solution.py:48
  240.0 23.1 %copy-start.2 = (bf16[1,4,32,256]{3,2,1,0:T(8,128)(2,1)S(1)}, bf16[1,4,32,256]{3,2,1,0:T(8,128)(2,1)}, u32[]{:S(2)}) copy-start(bf16[1,4,32,256]{3,2,1,0:T(8,128)(2,1)} %param.11) | copy-start | bytes 196612
  240.0 33.6 %copy-start.4 = (bf16[4,32,4,64]{3,2,1,0:T(4,128)(2,1)S(1)}, bf16[4,32,4,64]{3,2,1,0:T(4,128)(2,1)}, u32[]{:S(2)}) copy-start(bf16[4,32,4,64]{3,2,1,0:T(4,128)(2,1)} %copy-done.3) | copy-start | bytes 196612
  240.0 33.6 %copy-start.11 = (bf16[4,32,4,64]{3,2,1,0:T(4,128)(2,1)S(1)}, bf16[4,32,4,64]{3,2,1,0:T(4,128)(2,1)}, u32[]{:S(2)}) copy-start(bf16[4,32,4,64]{3,2,1,0:T(4,128)(2,1)} %copy-done.10) | copy-start | bytes 196612
  240.0 33.6 %copy-start.22 = (f32[4,32]{1,0:T(4,128)S(1)}, f32[4,32]{1,0:T(4,128)}, u32[]{:S(2)}) copy-start(f32[4,32]{1,0:T(4,128)} %get-tuple-element.17) | copy-start | bytes 1540
  240.0 33.6 %copy-start.26 = (pred[4,32]{1,0:T(4,128)(4,1)S(1)}, pred[4,32]{1,0:T(4,128)(4,1)}, u32[]{:S(2)}) copy-start(pred[4,32]{1,0:T(4,128)(4,1)} %get-tuple-element.16) | copy-start | bytes 388
  240.0 33.6 %copy-start.31 = (f32[4,4,32]{2,1,0:T(4,128)S(1)}, f32[4,4,32]{2,1,0:T(4,128)}, u32[]{:S(2)}) copy-start(f32[4,4,32]{2,1,0:T(4,128)} %copy-done.30) | copy-start | bytes 6148
  264.7 21.3 %all-to-all-start.3 = ((f32[16,1,128]{2,1,0:T(1,128)}), f32[16,1,128]{2,1,0:T(1,128)S(1)}, u32[]{:S(2)}, u32[]{:S(2)}) async-start(f32[16,1,128]{2,1,0:T(1,128)} %reshape.194), calls=%async_computation.4 | async-start | bytes 16384 | tf_op jit(solution)/shard_map/all_to_all | solution.py:14
  286.0 18.6 %all-to-all-start.5 = ((f32[16,4,4,256]{3,2,1,0:T(4,128)}), f32[16,4,4,256]{3,2,1,0:T(4,128)S(1)}, u32[]{:S(2)}, u32[]{:S(2)}) async-start(f32[16,4,4,256]{3,2,1,0:T(4,128)} %bitcast.97), calls=%async_computation.6 | async-start | bytes 524288 | tf_op jit(solution)/shard_map/all_to_all | solution.py:48
  292.1 12.6 %copy-start.12 = (bf16[4,4,256]{2,1,0:T(4,128)(2,1)S(1)}, bf16[4,4,256]{2,1,0:T(4,128)(2,1)}, u32[]{:S(2)}) copy-start(bf16[4,4,256]{2,1,0:T(4,128)(2,1)} %param.12) | copy-start | bytes 24580
  292.2 19.4 %copy-start.8 = (bf16[4,32,256]{2,1,0:T(8,128)(2,1)S(1)}, bf16[4,32,256]{2,1,0:T(8,128)(2,1)}, u32[]{:S(2)}) copy-start(bf16[4,32,256]{2,1,0:T(8,128)(2,1)} %reduce-scatter.2.cloned.1.call-done) | copy-start | bytes 196612
  292.2 19.4 %copy-start.16 = (f32[4,32]{1,0:T(4,128)S(1)}, f32[4,32]{1,0:T(4,128)}, u32[]{:S(2)}) copy-start(f32[4,32]{1,0:T(4,128)} %copy-done.15) | copy-start | bytes 1540
  292.2 19.4 %copy-start.20 = (f32[4,32]{1,0:T(4,128)S(1)}, f32[4,32]{1,0:T(4,128)}, u32[]{:S(2)}) copy-start(f32[4,32]{1,0:T(4,128)} %get-tuple-element.8) | copy-start | bytes 1540
  305.4 18.8 %all-to-all-start.6 = ((f32[16,4,4,1]{2,1,3,0:T(4,128)}), f32[16,4,4,1]{2,1,3,0:T(4,128)S(1)}, u32[]{:S(2)}, u32[]{:S(2)}) async-start(f32[16,4,4,1]{2,1,3,0:T(4,128)} %broadcast_in_dim.87), calls=%async_computation.7 | async-start | bytes 65536 | tf_op jit(solution)/shard_map/all_to_all | solution.py:14
  (9 other events, 25.9 us)
Sparse Core Ops, SparseCore 0:
  38.1 58.7 all-gather.1
  194.6 68.4 reduce-scatter.1
where the time goes:
time: 333 us; the launch traced here: 332 us
  waiting for transfers between devices  130 us (39%)
  local copies, waits for them, and re-layouts  56.9 us (17%)
  starting transfers between devices  51.6 us (15%)
  blocking collectives  34.3 us (10%)
  matrix products  30.5 us (9%)
  between operations  14.6 us (4%)
  other arithmetic  13.3 us (4%)
    all_to_all x4, waiting for transfers between devices, sent_to_all(): return lax.all_to_all(copies, axis, split_axis=0, concat_axis=0, tiled=True)  98.8 us
    all_to_all x4, starting transfers between devices, sent_to_all(): return lax.all_to_all(copies, axis, split_axis=0, concat_axis=0, tiled=True)  36.2 us
    reduce_scatter x1, waiting for transfers between devices, shards(): lax.psum_scatter(normed_part.astype(jnp.bfloat16), 'tp', scatter_dimensio...  21.8 us
    all_gather x1, blocking collectives, sent_together(): out = lax.all_gather(both, axis, axis=dim, tiled=True)  21.7 us
    unnamed x71, local copies, waits for them, and re-layouts  16.8 us
    convert_element_type x5, local copies, waits for them, and re-layouts, normalize(): floats = hidden_in.astype(jnp.float32)  13.8 us
    all_to_all x1, blocking collectives, sent_to_all(): return lax.all_to_all(copies, axis, split_axis=0, concat_axis=0, tiled=True)  12.6 us
    all_to_all x2, starting transfers between devices, summed_on_arrival(): lax.all_to_all(pieces, axis, split_axis=0, concat_axis=0, tiled=True)  11.2 us
  transfers between devices with their start and end apart: 9, of which 6 were waited for; matrix products, arithmetic and copies ran while one was open for 29% of the time, Pallas kernels for 0%

commit v1 on v0

v1 whole, which is shorter than its diff:
```python
import functools

import jax
import jax.numpy as jnp
from jax import lax
from jax.experimental import pallas as pl
from jax.experimental.pallas import tpu as pltpu
from jax.sharding import PartitionSpec as P

MESH = pl.DeviceIdType.MESH
F32 = jnp.float32
BF16 = jnp.bfloat16
EPSILON = 1e-06
HEAD_DIM = 64
N_SECTION = 8
N_TP = 16
N_DP = 4
ROWS = 128
WIDE = 256
HALF = 64
PIECE = 16
FIRST_DECODER = N_SECTION // 2
WAYS = [(0, 0), (1, 0), (0, 1), (1, 1)]


def dot_nn(a, b):
    return lax.dot_general(a, b, (((1,), (0,)), ((), ())), preferred_element_type=F32)


def dot_nt(a, b):
    return lax.dot_general(a, b, (((1,), (1,)), ((), ())), preferred_element_type=F32)


def dot_tn(a, b):
    return lax.dot_general(a, b, (((0,), (0,)), ((), ())), preferred_element_type=F32)


def hops(way):
    return N_TP // 2 if way[0] == way[1] else N_TP // 2 - 1


def body(
    stream, mem, lgain, fgain, wq, wk, wv, cot, enc_len, dec_len, assign,
    mix_o, sg_o, mg_o, dq_o, dk_o, dv_o,
    piece, gat, xm, wf, acc, inv, g_own, g_all, x_all, x_rel, part, rs, dots, rsd, h_out, h_in,
    ag_s, ag_r, wy_s, wy_r, wc_s, wc_r, wr_s, wr_r, m_s, m_r, ex_s, ex_r, rs_s, rs_r, d_s, d_r, h_s, h_r, loc,
):
    s = lax.axis_index("section")
    z = lax.axis_index("tp")
    d = lax.axis_index("dp")
    is_dec = s >= FIRST_DECODER
    src = jnp.where(is_dec, 1, 0)
    core = lax.rem(d, 2)
    chip = lax.div(d, 2)
    mate = d + 1 - 2 * core
    far = lax.rem(d + 2, N_DP)
    far_mate = lax.rem(mate + 2, N_DP)
    right = {"tp": lax.rem(z + 1, N_TP)}
    left = {"tp": lax.rem(z + N_TP - 1, N_TP)}
    around = [right, left]

    def remote(a, b, ss, rr, to):
        return pltpu.make_async_remote_copy(
            src_ref=a, dst_ref=b, send_sem=ss, recv_sem=rr, device_id=to, device_id_type=MESH
        )

    barrier = pltpu.get_barrier_semaphore()
    for to in (right, left, {"dp": mate}, {"dp": far}):
        pl.semaphore_signal(barrier, inc=1, device_id=to, device_id_type=MESH)
    for other in range(1, N_SECTION):
        pl.semaphore_signal(
            barrier, inc=1, device_id={"section": lax.rem(s + other, N_SECTION)}, device_id_type=MESH
        )

    own = [
        pltpu.make_async_copy(stream, gat.at[0, z], loc.at[0]),
        pltpu.make_async_copy(wq, wf.at[0, pl.ds(4 * d, 4)], loc.at[1]),
        pltpu.make_async_copy(wk, wf.at[1, pl.ds(4 * d, 4)], loc.at[2]),
        pltpu.make_async_copy(wv, wf.at[2, pl.ds(4 * d, 4)], loc.at[3]),
    ]
    for c in own[1:]:
        c.start()
    own[0].start()
    piece[...] = jnp.concatenate([mem[n].astype(F32) for n in range(4)], axis=0).astype(BF16)
    pl.semaphore_wait(barrier, N_SECTION + 3)

    def ring(which, way, k):
        direction, chunk = way
        rows = pl.ds(chunk * HALF, HALF)
        back = k - 1 if direction == 0 else 1 - k
        at = lax.rem(z - back + N_TP, N_TP)
        return remote(
            gat.at[which, at, rows], gat.at[which, at, rows],
            ag_s.at[which, direction, chunk, k - 1], ag_r.at[which, direction, chunk, k - 1],
            around[direction],
        )

    def weight_far(w):
        return remote(
            wf.at[w, pl.ds(4 * d, 4)], wf.at[w, pl.ds(4 * d, 4)], wy_s.at[w], wy_r.at[w], {"dp": far}
        )

    def weight_mate(w):
        return remote(
            wf.at[w, pl.ds(4 * d, 4)], wf.at[w, pl.ds(4 * d, 4)], wc_s.at[w], wc_r.at[w], {"dp": mate}
        )

    def weight_relay(w):
        return remote(
            wf.at[w, pl.ds(4 * far, 4)], wf.at[w, pl.ds(4 * far, 4)], wr_s.at[w], wr_r.at[w], {"dp": mate}
        )

    own[0].wait()
    for way in WAYS:
        ring(0, way, 1).start()
    for w in range(3):
        own[1 + w].wait()
        weight_far(w).start()

    def mem_send(i):
        return remote(
            piece, gat.at[1, z, pl.ds(s * PIECE, PIECE)], m_s.at[i], m_r.at[0], {"section": FIRST_DECODER + i}
        )

    def mem_keep():
        return pltpu.make_async_copy(piece, gat.at[1, z, pl.ds(s * PIECE, PIECE)], m_r.at[0])

    for i in range(N_SECTION - FIRST_DECODER):
        @pl.when(s != FIRST_DECODER + i)
        def _():
            mem_send(i).start()

    @pl.when(is_dec)
    def _():
        mem_keep().start()

    for w in range(3):
        weight_mate(w).start()

    @pl.when(is_dec)
    def _():
        pltpu.make_async_copy(gat.at[1, z], gat.at[1, z], m_r.at[0]).wait()
        for way in WAYS:
            ring(1, way, 1).start()

    def ring_step(k, _):
        for which in range(2):
            def go():
                for way in WAYS:
                    ring(which, way, k - 1).wait_recv()
                    if hops(way) == N_TP // 2:
                        ring(which, way, k).start()
                    else:
                        @pl.when(k < N_TP // 2)
                        def _():
                            ring(which, way, k).start()
            if which == 0:
                go()
            else:
                pl.when(is_dec)(go)
        return 0

    lax.fori_loop(2, 6, ring_step, 0)
    weight_far(0).wait_recv()
    weight_relay(0).start()
    lax.fori_loop(6, N_TP // 2 + 1, ring_step, 0)
    for way in WAYS:
        if hops(way) == N_TP // 2:
            ring(0, way, N_TP // 2).wait_recv()

    @pl.when(is_dec)
    def _():
        for way in WAYS:
            if hops(way) == N_TP // 2:
                ring(1, way, N_TP // 2).wait_recv()

    weight_far(1).wait_recv()
    weight_relay(1).start()

    def scaled(which, gain):
        def step(i, total):
            value = gat[which, i].astype(F32)
            wide = gain[0:1, pl.ds(pl.multiple_of(i * WIDE, WIDE), WIDE)]
            xm[which, i] = (value * wide).astype(BF16)
            return total + value * value

        total = lax.fori_loop(0, N_TP, step, jnp.zeros((ROWS, WIDE), F32))
        mean = jnp.sum(total, axis=1, keepdims=True) * (1.0 / (N_TP * WIDE))
        return jnp.broadcast_to(lax.rsqrt(mean + EPSILON), (ROWS, 128))

    stream_inverse = scaled(0, lgain)
    inv[0] = stream_inverse
    inv[1] = stream_inverse

    @pl.when(is_dec)
    def _():
        inv[1] = scaled(1, fgain)

    def project(w, begin, start):
        side = 0 if w == 0 else src

        def step(i, total):
            return total + dot_nn(xm[side, begin + i], wf[w, begin + i])

        acc[w] = lax.fori_loop(0, N_TP // 2, step, start)

    for w in range(3):
        weight_mate(w).wait_recv()
        project(w, chip * (N_TP // 2), jnp.zeros((ROWS, WIDE), F32))
    for w in range(3):
        if w == 2:
            weight_far(2).wait_recv()
            weight_relay(2).start()
        weight_relay(w).wait_recv()
        project(w, (1 - chip) * (N_TP // 2), acc[w])

    def give_far(side):
        return remote(
            xm.at[side, pl.ds(4 * far, 4)], x_all.at[side, :, d], ex_s.at[side, 0], ex_r.at[side, 0], {"dp": far}
        )

    def give_far_mate(side):
        return remote(
            xm.at[side, pl.ds(4 * far_mate, 4)], x_rel.at[side], ex_s.at[side, 1], ex_r.at[side, 1], {"dp": far}
        )

    def give_mate(side):
        return remote(
            xm.at[side, pl.ds(4 * mate, 4)], x_all.at[side, :, d], ex_s.at[side, 2], ex_r.at[side, 2], {"dp": mate}
        )

    def relay_mate(side):
        return remote(
            x_rel.at[side], x_all.at[side, :, far], ex_s.at[side, 3], ex_r.at[side, 3], {"dp": mate}
        )

    def keep_own(side):
        return pltpu.make_async_copy(xm.at[side, pl.ds(4 * d, 4)], x_all.at[side, :, d], loc.at[4 + side])

    def start_exchange(side):
        give_far_mate(side).start()
        give_far(side).start()
        give_mate(side).start()
        keep_own(side).start()

    start_exchange(0)

    @pl.when(is_dec)
    def _():
        start_exchange(1)

    row = lax.broadcasted_iota(jnp.int32, (ROWS, ROWS), 0)
    col = lax.broadcasted_iota(jnp.int32, (ROWS, ROWS), 1)
    row_sample = lax.shift_right_logical(row, 5)
    col_sample = jnp.where(
        is_dec, jnp.bitwise_and(lax.shift_right_logical(col, 2), 3), lax.shift_right_logical(col, 5)
    )
    col_slot = jnp.where(
        is_dec, lax.shift_right_logical(col, 4) * 4 + jnp.bitwise_and(col, 3), jnp.bitwise_and(col, 31)
    )
    wanted = jnp.zeros((ROWS, ROWS), jnp.int32)
    key_len = jnp.zeros((ROWS, ROWS), jnp.int32)
    query_len = jnp.zeros((ROWS, ROWS), jnp.int32)
    for m in range(4):
        chosen = jnp.where(is_dec, assign[m], m)
        length = jnp.where(is_dec, dec_len[m], enc_len[m])
        wanted = jnp.where(row_sample == m, chosen, wanted)
        key_len = jnp.where(col_sample == m, enc_len[m], key_len)
        query_len = jnp.where(row_sample == m, length, query_len)
    live = jnp.logical_and(wanted == col_sample, col_slot < key_len)
    row_live = (jnp.bitwise_and(row, 31) < query_len).astype(F32)[:, 0:HEAD_DIM]

    q_scale = jnp.concatenate([inv[0], inv[0]], axis=1)
    s_scale = jnp.concatenate([inv[1], inv[1]], axis=1)
    queries = (acc[0] * q_scale).astype(BF16)
    keys = (acc[1] * s_scale).astype(BF16)
    values = (acc[2] * s_scale).astype(BF16)
    scale = HEAD_DIM**-0.5
    for h in range(WIDE // HEAD_DIM):
        at = slice(h * HEAD_DIM, (h + 1) * HEAD_DIM)
        qh, kh, vh = queries[:, at], keys[:, at], values[:, at]
        scores = jnp.where(live, dot_nt(qh, kh) * scale, -1e30)
        raised = jnp.exp(scores - jnp.max(scores, axis=1, keepdims=True))
        weights = raised / jnp.sum(raised, axis=1, keepdims=True)
        probs = weights.astype(BF16)
        mix_o[:, at] = (dot_nn(probs, vh) * row_live).astype(BF16)
        upstream = (cot[:, at].astype(F32) * row_live).astype(BF16)
        grad_weights = dot_nt(upstream, vh)
        inner = jnp.sum(grad_weights * weights, axis=1, keepdims=True)
        grad_scores = (weights * (grad_weights - inner) * scale).astype(BF16)
        g_own[0, :, at] = (dot_nn(grad_scores, kh) * inv[0][:, 0:HEAD_DIM]).astype(BF16)
        g_own[1, :, at] = (dot_tn(grad_scores, qh) * inv[1][:, 0:HEAD_DIM]).astype(BF16)
        g_own[2, :, at] = (dot_tn(probs, upstream) * inv[1][:, 0:HEAD_DIM]).astype(BF16)

    shared_dot = g_own[1].astype(F32) * acc[1] + g_own[2].astype(F32) * acc[2]
    query_dot = g_own[0].astype(F32) * acc[0]
    diagonal = row == col
    for side, total in ((0, jnp.where(is_dec, query_dot, query_dot + shared_dot)), (1, shared_dot)):
        column = jnp.sum(total, axis=1, keepdims=True) * (1.0 / (N_TP * WIDE)) * inv[side] * inv[side]
        across = jnp.sum(jnp.where(diagonal, column, 0.0), axis=0, keepdims=True)
        dots[:, side * 128 : (side + 1) * 128] = jnp.broadcast_to(across, (8, 128))

    def back(i):
        grad_q = dot_nt(g_own[0], wf[0, i])
        grad_s = dot_nt(g_own[1], wf[1, i]) + dot_nt(g_own[2], wf[2, i])
        part[0, i] = jnp.where(is_dec, grad_q, grad_q + grad_s).astype(BF16)
        part[1, i] = grad_s.astype(BF16)

    def chain_at(way_hops, direction, k):
        ahead = way_hops + 1 - k
        return lax.rem(z + ahead, N_TP) if direction == 0 else lax.rem(z - ahead + N_TP, N_TP)

    def chain(side, way, k, first):
        direction, chunk = way
        rows = pl.ds(chunk * HALF, HALF)
        begin = (
            part.at[side, chain_at(hops(way), direction, k), rows] if first else rs.at[side, direction, k - 2, rows]
        )
        return remote(
            begin, rs.at[side, direction, k - 1, rows],
            rs_s.at[side, direction, chunk, k - 1], rs_r.at[side, direction, chunk, k - 1], around[direction],
        )

    def chain_dots(direction, k, first):
        begin = dots if first else rsd.at[direction, k - 2]
        return remote(begin, rsd.at[direction, k - 1], d_s.at[direction, k - 1], d_r.at[direction, k - 1], around[direction])

    half = N_TP // 2
    back(lax.rem(z + half, N_TP))
    back(lax.rem(z + half - 1, N_TP))
    back(lax.rem(z + half + 1, N_TP))

    def chain_first(side):
        for way in WAYS:
            chain(side, way, 1, True).start()

    @pl.when(is_dec)
    def _():
        chain_first(1)

    chain_first(0)
    chain_dots(0, 1, True).start()
    chain_dots(1, 1, True).start()

    def g_far():
        return remote(g_own, g_all.at[:, d], ex_s.at[2, 0], ex_r.at[2, 0], {"dp": far})

    def g_mate():
        return remote(g_own, g_all.at[:, d], ex_s.at[2, 2], ex_r.at[2, 2], {"dp": mate})

    def g_relay():
        return remote(g_all.at[:, far], g_all.at[:, far], ex_s.at[2, 3], ex_r.at[2, 3], {"dp": mate})

    g_keep = pltpu.make_async_copy(g_own, g_all.at[:, d], loc.at[6])
    g_far().start()
    g_mate().start()
    g_keep.start()

    def chain_step(k, _):
        back(lax.rem(z + half - k, N_TP))

        @pl.when(k < half)
        def _():
            back(lax.rem(z + half + k, N_TP))

        def go(side):
            for way in WAYS:
                direction, chunk = way
                last = hops(way)

                def one():
                    chain(side, way, k - 1, True).wait_recv()
                    rows = pl.ds(chunk * HALF, HALF)
                    target = chain_at(last, direction, k)
                    rs[side, direction, k - 2, rows] = (
                        rs[side, direction, k - 2, rows].astype(F32) + part[side, target, rows].astype(F32)
                    ).astype(BF16)
                    chain(side, way, k, False).start()

                if last == N_TP // 2:
                    one()
                else:
                    pl.when(k < N_TP // 2)(one)

        pl.when(is_dec)(lambda: go(1))
        go(0)
        for direction in range(2):
            def one_dots():
                chain_dots(direction, k - 1, True).wait_recv()
                rsd[direction, k - 2] = rsd[direction, k - 2] + dots[...]
                chain_dots(direction, k, False).start()

            if direction == 0:
                one_dots()
            else:
                pl.when(k < N_TP // 2)(one_dots)
        return 0

    def relay(side):
        give_far_mate(side).wait_recv()
        relay_mate(side).start()

    def settled(side):
        give_far(side).wait_recv()
        give_mate(side).wait_recv()
        relay_mate(side).wait_recv()
        keep_own(side).wait()

    def weight_gradient(w, side, out):
        for j in range(4):
            left_side = x_all[side, j].reshape(N_DP * ROWS, WIDE)
            right_side = g_all[w].reshape(N_DP * ROWS, WIDE)
            out[j] = dot_tn(left_side, right_side).astype(BF16)

    lax.fori_loop(2, 6, chain_step, 0)
    g_far().wait_recv()
    g_relay().start()
    relay(0)
    lax.fori_loop(6, 8, chain_step, 0)
    pl.when(is_dec)(lambda: relay(1))
    settled(0)
    g_mate().wait_recv()
    g_relay().wait_recv()
    g_keep.wait()
    weight_gradient(0, 0, dq_o)
    lax.fori_loop(8, N_TP // 2 + 1, chain_step, 0)
    chain_dots(0, N_TP // 2, True).wait_recv()
    chain_dots(1, N_TP // 2 - 1, True).wait_recv()
    summed = rsd[0, N_TP // 2 - 1] + rsd[1, N_TP // 2 - 2] + dots[...]

    def arrived(side, chunk):
        rows = pl.ds(chunk * HALF, HALF)
        total = part[side, z, rows].astype(F32)
        for direction in range(2):
            way = (direction, chunk)
            chain(side, way, hops(way), True).wait_recv()
            total = total + rs[side, direction, hops(way) - 1, rows].astype(F32)
        return total

    def column_of(side):
        across = jnp.broadcast_to(summed[0:1, side * 128 : (side + 1) * 128], (ROWS, ROWS))
        return jnp.sum(jnp.where(diagonal, across, 0.0), axis=1, keepdims=True)

    here = pl.ds(pl.multiple_of(z * WIDE, WIDE), WIDE)

    def give_memory(i):
        return remote(h_out.at[i], h_in.at[s - FIRST_DECODER], h_s.at[i], h_r.at[0], {"section": i})

    @pl.when(is_dec)
    def _():
        gain = fgain[0:1, here]
        column = column_of(1)
        for chunk in range(2):
            rows = slice(chunk * HALF, (chunk + 1) * HALF)
            value = gain * arrived(1, chunk) - gat[1, z, rows].astype(F32) * column[rows]
            h_out[chunk * 4 : chunk * 4 + 4] = value.reshape(4, PIECE, WIDE)
        for i in range(N_SECTION):
            @pl.when(s != i)
            def _():
                give_memory(i).start()
        pltpu.make_async_copy(h_out.at[s], h_in.at[s - FIRST_DECODER], h_r.at[0]).start()

    gain_here = lgain[0:1, here]
    stream_column = column_of(0)
    for chunk in range(2):
        rows = slice(chunk * HALF, (chunk + 1) * HALF)
        value = gain_here * arrived(0, chunk) - stream[rows].astype(F32) * stream_column[rows]
        sg_o[rows] = value.astype(BF16)

    pl.when(is_dec)(lambda: settled(1))
    weight_gradient(1, src, dk_o)
    weight_gradient(2, src, dv_o)

    pltpu.make_async_copy(h_in, h_in, h_r.at[0]).wait()
    mg_o[...] = h_in[0] + h_in[1] + h_in[2] + h_in[3]

    def drain(which):
        for way in WAYS:
            def step(k, _):
                ring(which, way, k).wait_send()
                chain(which, way, k, True).wait_send()
                return 0

            lax.fori_loop(1, hops(way) + 1, step, 0)

    drain(0)
    pl.when(is_dec)(lambda: drain(1))
    for w in range(3):
        weight_far(w).wait_send()
        weight_mate(w).wait_send()
        weight_relay(w).wait_send()
    for i in range(N_SECTION - FIRST_DECODER):
        @pl.when(s != FIRST_DECODER + i)
        def _():
            mem_send(i).wait_send()

    def drain_exchange(side):
        give_far(side).wait_send()
        give_far_mate(side).wait_send()
        give_mate(side).wait_send()
        relay_mate(side).wait_send()

    drain_exchange(0)
    pl.when(is_dec)(lambda: drain_exchange(1))
    g_far().wait_send()
    g_mate().wait_send()
    g_relay().wait_send()
    for direction in range(2):
        def step(k, _):
            chain_dots(direction, k, True).wait_send()
            return 0

        lax.fori_loop(1, N_TP // 2 + 1 - direction, step, 0)

    @pl.when(is_dec)
    def _():
        for i in range(N_SECTION):
            @pl.when(s != i)
            def _():
                give_memory(i).wait_send()


def hand_out(mix, sg, mg, dq, dk, dv, mix_o, sg_o, mg_o, dq_o, dk_o, dv_o):
    mix_o[...] = mix[...]
    sg_o[...] = sg[...]
    for n in range(4):
        mg_o[n] = mg[n * 4 : n * 4 + 4].astype(BF16)
    dq_o[...] = dq[...]
    dk_o[...] = dk[...]
    dv_o[...] = dv[...]


def shards(
    stream, memory_hidden, layer_gain, final_gain, query_weight, key_weight, value_weight,
    cotangent, encoder_lengths, decoder_lengths, assignment,
):
    vmem = pl.BlockSpec(memory_space=pltpu.VMEM)
    hbm = pl.BlockSpec(memory_space=pl.ANY)
    smem = pl.BlockSpec(memory_space=pltpu.SMEM)
    dma = pltpu.SemaphoreType.DMA
    outs = pl.pallas_call(
        body,
        name="relay",
        out_shape=(
            jax.ShapeDtypeStruct((ROWS, WIDE), BF16),
            jax.ShapeDtypeStruct((ROWS, WIDE), BF16),
            jax.ShapeDtypeStruct((PIECE, WIDE), F32),
            jax.ShapeDtypeStruct((4, WIDE, WIDE), BF16),
            jax.ShapeDtypeStruct((4, WIDE, WIDE), BF16),
            jax.ShapeDtypeStruct((4, WIDE, WIDE), BF16),
        ),
        in_specs=[vmem, vmem, vmem, vmem, hbm, hbm, hbm, vmem, smem, smem, smem],
        out_specs=(vmem,) * 6,
        scratch_shapes=[
            pltpu.VMEM((PIECE, WIDE), BF16),
            pltpu.VMEM((2, N_TP, ROWS, WIDE), BF16),
            pltpu.VMEM((2, N_TP, ROWS, WIDE), BF16),
            pltpu.VMEM((3, N_TP, WIDE, WIDE), BF16),
            pltpu.VMEM((3, ROWS, WIDE), F32),
            pltpu.VMEM((2, ROWS, 128), F32),
            pltpu.VMEM((3, ROWS, WIDE), BF16),
            pltpu.VMEM((3, N_DP, ROWS, WIDE), BF16),
            pltpu.VMEM((2, 4, N_DP, ROWS, WIDE), BF16),
            pltpu.VMEM((2, 4, ROWS, WIDE), BF16),
            pltpu.VMEM((2, N_TP, ROWS, WIDE), BF16),
            pltpu.VMEM((2, 2, N_TP // 2, ROWS, WIDE), BF16),
            pltpu.VMEM((8, 256), F32),
            pltpu.VMEM((2, N_TP // 2, 8, 256), F32),
            pltpu.VMEM((N_SECTION, PIECE, WIDE), F32),
            pltpu.VMEM((N_SECTION - FIRST_DECODER, PIECE, WIDE), F32),
            dma((2, 2, 2, 8)), dma((2, 2, 2, 8)),
            dma((3,)), dma((3,)), dma((3,)), dma((3,)), dma((3,)), dma((3,)),
            dma((4,)), dma((1,)),
            dma((3, 4)), dma((3, 4)),
            dma((2, 2, 2, 8)), dma((2, 2, 2, 8)),
            dma((2, 8)), dma((2, 8)),
            dma((8,)), dma((1,)),
            dma((7,)),
        ],
        compiler_params=pltpu.CompilerParams(
            collective_id=0, has_side_effects=True, vmem_limit_bytes=60 * 1024 * 1024
        ),
    )(
        stream.reshape(ROWS, WIDE),
        memory_hidden,
        layer_gain,
        final_gain.reshape(1, N_TP * WIDE),
        query_weight.reshape(4, WIDE, WIDE),
        key_weight.reshape(4, WIDE, WIDE),
        value_weight.reshape(4, WIDE, WIDE),
        cotangent.reshape(ROWS, WIDE),
        encoder_lengths,
        decoder_lengths,
        assignment.reshape(4),
    )
    mixture, stream_grad, memory_grad, dq, dk, dv = pl.pallas_call(
        hand_out,
        name="hand_out",
        out_shape=(
            jax.ShapeDtypeStruct((ROWS, WIDE), BF16),
            jax.ShapeDtypeStruct((ROWS, WIDE), BF16),
            jax.ShapeDtypeStruct((4, 4, WIDE), BF16),
            jax.ShapeDtypeStruct((4, WIDE, WIDE), BF16),
            jax.ShapeDtypeStruct((4, WIDE, WIDE), BF16),
            jax.ShapeDtypeStruct((4, WIDE, WIDE), BF16),
        ),
        in_specs=[vmem] * 6,
        out_specs=(vmem,) * 6,
    )(*outs)
    rows = (1, 4, 32, WIDE)
    square = (1, 4 * WIDE, WIDE)
    return (
        mixture.reshape(rows),
        stream_grad.reshape(rows),
        memory_grad,
        dq.reshape(square),
        dk.reshape(square),
        dv.reshape(square),
    )


def solution(mesh):
    tokens = P("section", "dp", None, "tp")
    weight = P("section", "dp", "tp")
    memory = P("dp", "section", "tp")
    return jax.shard_map(
        shards,
        mesh=mesh,
        in_specs=(
            tokens, memory, P("section", None), P(), weight, weight, weight, tokens, P("dp"), P("dp"), P("dp", None),
        ),
        out_specs=(tokens, tokens, memory, weight, weight, weight),
        check_vma=False,
    )
```

time: 333 us -> 141 us (0.42)
  Pallas kernels: 0 us -> 139 us
  waiting for transfers between devices: 130 us -> 0 us
  local copies, waits for them, and re-layouts: 56.9 us -> 0 us
  starting transfers between devices: 51.6 us -> 0 us
  blocking collectives: 34.3 us -> 0 us
  matrix products: 30.5 us -> 0 us
  between operations: 14.6 us -> 0.64 us
  other arithmetic: 13.3 us -> 0 us
    pallas_call x0 -> x2, Pallas kernels: none -> 139 us  [the longest x1 137 us: shards(): pl.pallas_call(body, name='relay', out_shape=(jax.ShapeDtypeStruct((ROWS,...]
    all_to_all x7 -> x0, waiting for transfers between devices: 109 us -> none  [the longest x4 98.8 us: sent_to_all(): return lax.all_to_all(copies, axis, split_axis=0, concat_axis=0, tiled=True)]
    all_to_all x7 -> x0, starting transfers between devices: 51.6 us -> none  [the longest x4 36.2 us: sent_to_all(): return lax.all_to_all(copies, axis, split_axis=0, concat_axis=0, tiled=True)]
    dot_general x16 -> x0, matrix products: 30.2 us -> none  [the longest x3 9.69 us: contract_last(): lax.dot_general(left, right, (((1,), (1,)), ((), ())), preferred_element_...]
    reduce_scatter x1 -> x0, waiting for transfers between devices: 21.8 us -> none  [shards(): lax.psum_scatter(normed_part.astype(jnp.bfloat16), 'tp', scatter_dimensio...]
    all_gather x1 -> x0, blocking collectives: 21.7 us -> none  [sent_together(): out = lax.all_gather(both, axis, axis=dim, tiled=True)]
    unnamed x71 -> x0, local copies, waits for them, and re-layouts: 16.8 us -> none
    convert_element_type x10 -> x0, local copies, waits for them, and re-layouts: 14.2 us -> none  [the longest x5 13.8 us: normalize(): floats = hidden_in.astype(jnp.float32)]
  transfers between devices with their start and end apart: 9 -> 0, of which waited for: 6 -> 0; matrix products, arithmetic and copies ran while one was open for 29% -> 0% of each run, Pallas kernels for 0% -> 0%
where the time goes in v1:
time: 141 us; the launch traced here: 140 us
  Pallas kernels  139 us (99%)
    pallas_call x1, Pallas kernels, shards(): pl.pallas_call(body, name='relay', out_shape=(jax.ShapeDtypeStruct((ROWS,...  137 us

profile of v1, /device:TPU:6, one launch (start us, length us, event | category | flops | bytes accessed | tf_op | source)
XLA Modules:
  0.0 140.1 jit_solution(4846195544836065660)
XLA Ops:
  0.6 136.8 %relay.1 = (bf16[128,256]{1,0:T(8,128)(2,1)}, bf16[128,256]{1,0:T(8,128)(2,1)}, f32[16,256]{1,0:T(8,128)}, bf16[4,256,256]{2,1,0:T(8,128)(2,1)}, bf16[4,256,256]...) custom-call(bf16[128,256]{1,0:T(8,128)(2,1)} %bitcast.15, bf16[4,4,256]{2,1,0:T(4,128)(2,1)} %mem.1, f32[1,4096]{1,0:T(1,128)} %lgain.1, ...), custom_call_target="tpu_custom_call" | custom-call | tf_op jit(solution)/shard_map/relay/pallas_call | solution.py:541
  137.4 2.6 %hand_out.1 = (bf16[128,256]{1,0:T(8,128)(2,1)}, bf16[128,256]{1,0:T(8,128)(2,1)}, bf16[4,4,256]{2,1,0:T(4,128)(2,1)}, bf16[4,256,256]{2,1,0:T(8,128)(2,1)}, bf1...) custom-call(bf16[128,256]{1,0:T(8,128)(2,1)} %get-tuple-element.18.mix, bf16[128,256]{1,0:T(8,128)(2,1)} %get-tuple-element.19.sg, ...), custom_call_target="tpu_custom_call" | custom-call | tf_op jit(solution)/shard_map/hand_out/pallas_call | solution.py:596

commit v2 on v1

--- a/solution.py
+++ b/solution.py
@@ -110,29 +110,29 @@
             wf.at[w, pl.ds(4 * far, 4)], wf.at[w, pl.ds(4 * far, 4)], wr_s.at[w], wr_r.at[w], {"dp": mate}
         )
 
+    def mem_send(i):
+        return remote(
+            piece, gat.at[1, z, pl.ds(s * PIECE, PIECE)], m_s.at[i], m_r.at[0], {"section": FIRST_DECODER + i}
+        )
+
+    def mem_keep():
+        return pltpu.make_async_copy(piece, gat.at[1, z, pl.ds(s * PIECE, PIECE)], m_r.at[0])
+
+    for i in range(N_SECTION - FIRST_DECODER):
+        @pl.when(s != FIRST_DECODER + i)
+        def _():
+            mem_send(i).start()
+
+    @pl.when(is_dec)
+    def _():
+        mem_keep().start()
+
     own[0].wait()
     for way in WAYS:
         ring(0, way, 1).start()
     for w in range(3):
         own[1 + w].wait()
         weight_far(w).start()
-
-    def mem_send(i):
-        return remote(
-            piece, gat.at[1, z, pl.ds(s * PIECE, PIECE)], m_s.at[i], m_r.at[0], {"section": FIRST_DECODER + i}
-        )
-
-    def mem_keep():
-        return pltpu.make_async_copy(piece, gat.at[1, z, pl.ds(s * PIECE, PIECE)], m_r.at[0])
-
-    for i in range(N_SECTION - FIRST_DECODER):
-        @pl.when(s != FIRST_DECODER + i)
-        def _():
-            mem_send(i).start()
-
-    @pl.when(is_dec)
-    def _():
-        mem_keep().start()
 
     for w in range(3):
         weight_mate(w).start()

time: 141 us -> 109 us (0.77)
  Pallas kernels: 139 us -> 107 us
    pallas_call x1, Pallas kernels: 137 us -> 105 us  [shards(): pl.pallas_call(body, name='relay', out_shape=(jax.ShapeDtypeStruct((ROWS,...]
where the time goes in v2:
time: 109 us; the launch traced here: 108 us
  Pallas kernels  107 us (98%)
    pallas_call x1, Pallas kernels, shards(): pl.pallas_call(body, name='relay', out_shape=(jax.ShapeDtypeStruct((ROWS,...  105 us
    pallas_call x1, Pallas kernels, shards(): pl.pallas_call(hand_out, name='hand_out', out_shape=(jax.ShapeDtypeStruct...  2.64 us

profile of v2, /device:TPU:6, one launch (start us, length us, event | category | flops | bytes accessed | tf_op | source)
XLA Modules:
  0.0 107.9 jit_solution(15739740023078843078)
XLA Ops:
  0.6 104.6 %relay.1 = (bf16[128,256]{1,0:T(8,128)(2,1)}, bf16[128,256]{1,0:T(8,128)(2,1)}, f32[16,256]{1,0:T(8,128)}, bf16[4,256,256]{2,1,0:T(8,128)(2,1)}, bf16[4,256,256]...) custom-call(bf16[128,256]{1,0:T(8,128)(2,1)} %bitcast.15, bf16[4,4,256]{2,1,0:T(4,128)(2,1)} %mem.1, f32[1,4096]{1,0:T(1,128)} %lgain.1, ...), custom_call_target="tpu_custom_call" | custom-call | tf_op jit(solution)/shard_map/relay/pallas_call | solution.py:541
  105.2 2.6 %hand_out.1 = (bf16[128,256]{1,0:T(8,128)(2,1)}, bf16[128,256]{1,0:T(8,128)(2,1)}, bf16[4,4,256]{2,1,0:T(4,128)(2,1)}, bf16[4,256,256]{2,1,0:T(8,128)(2,1)}, bf1...) custom-call(bf16[128,256]{1,0:T(8,128)(2,1)} %get-tuple-element.18.mix, bf16[128,256]{1,0:T(8,128)(2,1)} %get-tuple-element.19.sg, ...), custom_call_target="tpu_custom_call" | custom-call | tf_op jit(solution)/shard_map/hand_out/pallas_call | solution.py:596

commit v3 on v2

--- a/solution.py
+++ b/solution.py
@@ -42,7 +42,7 @@
 def body(
     stream, mem, lgain, fgain, wq, wk, wv, cot, enc_len, dec_len, assign,
     mix_o, sg_o, mg_o, dq_o, dk_o, dv_o,
-    piece, gat, xm, wf, acc, inv, g_own, g_all, x_all, x_rel, part, rs, dots, rsd, h_out, h_in,
+    piece, gat, xm, sq, wf, acc, inv, g_own, g_all, x_all, x_rel, part, rs, dots, rsd, h_out, h_in,
     ag_s, ag_r, wy_s, wy_r, wc_s, wc_r, wr_s, wr_r, m_s, m_r, ex_s, ex_r, rs_s, rs_r, d_s, d_r, h_s, h_r, loc,
 ):
     s = lax.axis_index("section")
@@ -82,6 +82,10 @@
         c.start()
     own[0].start()
     piece[...] = jnp.concatenate([mem[n].astype(F32) for n in range(4)], axis=0).astype(BF16)
+    for side in range(2):
+        sq[side] = jnp.zeros((ROWS, WIDE), F32)
+    for w in range(3):
+        acc[w] = jnp.zeros((ROWS, WIDE), F32)
     pl.semaphore_wait(barrier, N_SECTION + 3)
 
     def ring(which, way, k):
@@ -143,111 +147,145 @@
         for way in WAYS:
             ring(1, way, 1).start()
 
-    def ring_step(k, _):
+    half = N_TP // 2
+
+    def take(side, i):
+        value = gat[side, i].astype(F32)
+        gain = (lgain, fgain)[side][0:1, pl.ds(pl.multiple_of(i * WIDE, WIDE), WIDE)]
+        xm[side, i] = (value * gain).astype(BF16)
+        sq[side] = sq[side] + value * value
+
+    def near(side, i):
+        def add(w):
+            acc[w] = acc[w] + dot_nn(xm[side, i], wf[w, i])
+
+        @pl.when(lax.div(i, half) == chip)
+        def _():
+            if side == 0:
+                add(0)
+
+                @pl.when(jnp.logical_not(is_dec))
+                def _():
+                    add(1)
+                    add(2)
+            else:
+                add(1)
+                add(2)
+
+    def both_sides(f, i):
+        f(0, i)
+        pl.when(is_dec)(lambda: f(1, i))
+
+    def ring_step(k, multiply):
         for which in range(2):
             def go():
                 for way in WAYS:
                     ring(which, way, k - 1).wait_recv()
-                    if hops(way) == N_TP // 2:
+                    if hops(way) == half:
                         ring(which, way, k).start()
                     else:
-                        @pl.when(k < N_TP // 2)
+                        @pl.when(k < half)
                         def _():
                             ring(which, way, k).start()
             if which == 0:
                 go()
             else:
                 pl.when(is_dec)(go)
-        return 0
-
-    lax.fori_loop(2, 6, ring_step, 0)
+        for i in (lax.rem(z + N_TP + 1 - k, N_TP), lax.rem(z + k - 1, N_TP)):
+            both_sides(take, i)
+            if multiply:
+                both_sides(near, i)
+
+    def early(k, carry):
+        ring_step(k, False)
+        return carry
+
+    def later(k, carry):
+        ring_step(k, True)
+        return carry
+
+    both_sides(take, z)
+    lax.fori_loop(2, 4, early, 0)
+    for w in range(3):
+        weight_mate(w).wait_recv()
+    for distance in (0, 1, -1, 2, -2):
+        both_sides(near, lax.rem(z + distance + N_TP, N_TP))
+    lax.fori_loop(4, 6, later, 0)
     weight_far(0).wait_recv()
     weight_relay(0).start()
-    lax.fori_loop(6, N_TP // 2 + 1, ring_step, 0)
-    for way in WAYS:
-        if hops(way) == N_TP // 2:
-            ring(0, way, N_TP // 2).wait_recv()
+    lax.fori_loop(6, half + 1, later, 0)
+
+    def ring_end(side):
+        for way in WAYS:
+            if hops(way) == half:
+                ring(side, way, half).wait_recv()
+        opposite = lax.rem(z + half, N_TP)
+        take(side, opposite)
+        near(side, opposite)
+
+    ring_end(0)
+    pl.when(is_dec)(lambda: ring_end(1))
+    weight_far(1).wait_recv()
+    weight_relay(1).start()
+
+    def row_scale(side):
+        mean = jnp.sum(sq[side], axis=1, keepdims=True) * (1.0 / (N_TP * WIDE))
+        return jnp.broadcast_to(lax.rsqrt(mean + EPSILON), (ROWS, 128))
+
+    stream_inverse = row_scale(0)
+    inv[0] = stream_inverse
+    inv[1] = stream_inverse
 
     @pl.when(is_dec)
     def _():
-        for way in WAYS:
-            if hops(way) == N_TP // 2:
-                ring(1, way, N_TP // 2).wait_recv()
-
-    weight_far(1).wait_recv()
-    weight_relay(1).start()
-
-    def scaled(which, gain):
-        def step(i, total):
-            value = gat[which, i].astype(F32)
-            wide = gain[0:1, pl.ds(pl.multiple_of(i * WIDE, WIDE), WIDE)]
-            xm[which, i] = (value * wide).astype(BF16)
-            return total + value * value
-
-        total = lax.fori_loop(0, N_TP, step, jnp.zeros((ROWS, WIDE), F32))
-        mean = jnp.sum(total, axis=1, keepdims=True) * (1.0 / (N_TP * WIDE))
-        return jnp.broadcast_to(lax.rsqrt(mean + EPSILON), (ROWS, 128))
-
-    stream_inverse = scaled(0, lgain)
-    inv[0] = stream_inverse
-    inv[1] = stream_inverse
-
-    @pl.when(is_dec)
-    def _():
-        inv[1] = scaled(1, fgain)
-
-    def project(w, begin, start):
+        inv[1] = row_scale(1)
+
+    def give_far(side):
+        return remote(
+            xm.at[side, pl.ds(4 * far, 4)], x_all.at[side, :, d], ex_s.at[side, 0], ex_r.at[side, 0], {"dp": far}
+        )
+
+    def give_far_mate(side):
+        return remote(
+            xm.at[side, pl.ds(4 * far_mate, 4)], x_rel.at[side], ex_s.at[side, 1], ex_r.at[side, 1], {"dp": far}
+        )
+
+    def give_mate(side):
+        return remote(
+            xm.at[side, pl.ds(4 * mate, 4)], x_all.at[side, :, d], ex_s.at[side, 2], ex_r.at[side, 2], {"dp": mate}
+        )
+
+    def relay_mate(side):
+        return remote(
+            x_rel.at[side], x_all.at[side, :, far], ex_s.at[side, 3], ex_r.at[side, 3], {"dp": mate}
+        )
+
+    def keep_own(side):
+        return pltpu.make_async_copy(xm.at[side, pl.ds(4 * d, 4)], x_all.at[side, :, d], loc.at[4 + side])
+
+    def start_exchange(side):
+        give_far_mate(side).start()
+        give_far(side).start()
+        give_mate(side).start()
+        keep_own(side).start()
+
+    start_exchange(0)
+
+    def project(w):
         side = 0 if w == 0 else src
+        begin = (1 - chip) * half
 
         def step(i, total):
             return total + dot_nn(xm[side, begin + i], wf[w, begin + i])
 
-        acc[w] = lax.fori_loop(0, N_TP // 2, step, start)
-
-    for w in range(3):
-        weight_mate(w).wait_recv()
-        project(w, chip * (N_TP // 2), jnp.zeros((ROWS, WIDE), F32))
+        acc[w] = lax.fori_loop(0, half, step, acc[w])
+
     for w in range(3):
         if w == 2:
             weight_far(2).wait_recv()
             weight_relay(2).start()
         weight_relay(w).wait_recv()
-        project(w, (1 - chip) * (N_TP // 2), acc[w])
-
-    def give_far(side):
-        return remote(
-            xm.at[side, pl.ds(4 * far, 4)], x_all.at[side, :, d], ex_s.at[side, 0], ex_r.at[side, 0], {"dp": far}
-        )
-
-    def give_far_mate(side):
-        return remote(
-            xm.at[side, pl.ds(4 * far_mate, 4)], x_rel.at[side], ex_s.at[side, 1], ex_r.at[side, 1], {"dp": far}
-        )
-
-    def give_mate(side):
-        return remote(
-            xm.at[side, pl.ds(4 * mate, 4)], x_all.at[side, :, d], ex_s.at[side, 2], ex_r.at[side, 2], {"dp": mate}
-        )
-
-    def relay_mate(side):
-        return remote(
-            x_rel.at[side], x_all.at[side, :, far], ex_s.at[side, 3], ex_r.at[side, 3], {"dp": mate}
-        )
-
-    def keep_own(side):
-        return pltpu.make_async_copy(xm.at[side, pl.ds(4 * d, 4)], x_all.at[side, :, d], loc.at[4 + side])
-
-    def start_exchange(side):
-        give_far_mate(side).start()
-        give_far(side).start()
-        give_mate(side).start()
-        keep_own(side).start()
-
-    start_exchange(0)
-
-    @pl.when(is_dec)
-    def _():
-        start_exchange(1)
+        project(w)
 
     row = lax.broadcasted_iota(jnp.int32, (ROWS, ROWS), 0)
     col = lax.broadcasted_iota(jnp.int32, (ROWS, ROWS), 1)
@@ -325,7 +363,6 @@
         begin = dots if first else rsd.at[direction, k - 2]
         return remote(begin, rsd.at[direction, k - 1], d_s.at[direction, k - 1], d_r.at[direction, k - 1], around[direction])
 
-    half = N_TP // 2
     back(lax.rem(z + half, N_TP))
     back(lax.rem(z + half - 1, N_TP))
     back(lax.rem(z + half + 1, N_TP))
@@ -355,6 +392,7 @@
     g_far().start()
     g_mate().start()
     g_keep.start()
+    pl.when(is_dec)(lambda: start_exchange(1))
 
     def chain_step(k, _):
         back(lax.rem(z + half - k, N_TP))
@@ -417,7 +455,6 @@
     g_relay().start()
     relay(0)
     lax.fori_loop(6, 8, chain_step, 0)
-    pl.when(is_dec)(lambda: relay(1))
     settled(0)
     g_mate().wait_recv()
     g_relay().wait_recv()
@@ -467,6 +504,7 @@
         value = gain_here * arrived(0, chunk) - stream[rows].astype(F32) * stream_column[rows]
         sg_o[rows] = value.astype(BF16)
 
+    pl.when(is_dec)(lambda: relay(1))
     pl.when(is_dec)(lambda: settled(1))
     weight_gradient(1, src, dk_o)
     weight_gradient(2, src, dv_o)
@@ -520,14 +558,24 @@
                 give_memory(i).wait_send()
 
 
-def hand_out(mix, sg, mg, dq, dk, dv, mix_o, sg_o, mg_o, dq_o, dk_o, dv_o):
-    mix_o[...] = mix[...]
-    sg_o[...] = sg[...]
+def hand_out(mg, mix, sg, dq, dk, dv, mg_o, mix_o, sg_o, dq_o, dk_o, dv_o, small, large, sem):
+    places = (small.at[0], small.at[1], large.at[0], large.at[1], large.at[2])
+    taken = [
+        pltpu.make_async_copy(a, b, sem.at[0, n]) for n, (a, b) in enumerate(zip((mix, sg, dq, dk, dv), places))
+    ]
+    given = [
+        pltpu.make_async_copy(a, b, sem.at[1, n])
+        for n, (a, b) in enumerate(zip(places, (mix_o, sg_o, dq_o, dk_o, dv_o)))
+    ]
+    for c in taken:
+        c.start()
     for n in range(4):
         mg_o[n] = mg[n * 4 : n * 4 + 4].astype(BF16)
-    dq_o[...] = dq[...]
-    dk_o[...] = dk[...]
-    dv_o[...] = dv[...]
+    for a, b in zip(taken, given):
+        a.wait()
+        b.start()
+    for c in given:
+        c.wait()
 
 
 def shards(
@@ -555,6 +603,7 @@
             pltpu.VMEM((PIECE, WIDE), BF16),
             pltpu.VMEM((2, N_TP, ROWS, WIDE), BF16),
             pltpu.VMEM((2, N_TP, ROWS, WIDE), BF16),
+            pltpu.VMEM((2, ROWS, WIDE), F32),
             pltpu.VMEM((3, N_TP, WIDE, WIDE), BF16),
             pltpu.VMEM((3, ROWS, WIDE), F32),
             pltpu.VMEM((2, ROWS, 128), F32),
@@ -593,20 +642,26 @@
         decoder_lengths,
         assignment.reshape(4),
     )
-    mixture, stream_grad, memory_grad, dq, dk, dv = pl.pallas_call(
+    mixture, stream_grad, memory_grad, dq, dk, dv = outs
+    memory_grad, mixture, stream_grad, dq, dk, dv = pl.pallas_call(
         hand_out,
         name="hand_out",
         out_shape=(
+            jax.ShapeDtypeStruct((4, 4, WIDE), BF16),
             jax.ShapeDtypeStruct((ROWS, WIDE), BF16),
             jax.ShapeDtypeStruct((ROWS, WIDE), BF16),
-            jax.ShapeDtypeStruct((4, 4, WIDE), BF16),
             jax.ShapeDtypeStruct((4, WIDE, WIDE), BF16),
             jax.ShapeDtypeStruct((4, WIDE, WIDE), BF16),
             jax.ShapeDtypeStruct((4, WIDE, WIDE), BF16),
         ),
-        in_specs=[vmem] * 6,
-        out_specs=(vmem,) * 6,
-    )(*outs)
+        in_specs=[vmem] + [hbm] * 5,
+        out_specs=(vmem,) + (hbm,) * 5,
+        scratch_shapes=[
+            pltpu.VMEM((2, ROWS, WIDE), BF16),
+            pltpu.VMEM((3, 4, WIDE, WIDE), BF16),
+            dma((2, 5)),
+        ],
+    )(memory_grad, mixture, stream_grad, dq, dk, dv)
     rows = (1, 4, 32, WIDE)
     square = (1, 4 * WIDE, WIDE)
     return (

time: 109 us -> 98.4 us (0.903)
  Pallas kernels: 107 us -> 95.9 us
    pallas_call x1, Pallas kernels: 105 us -> 92.3 us  [shards(): pl.pallas_call(body, name='relay', out_shape=(jax.ShapeDtypeStruct((ROWS,...]
where the time goes in v3:
time: 98.4 us; the launch traced here: 96.6 us
  Pallas kernels  95.9 us (97%)
    pallas_call x1, Pallas kernels, shards(): pl.pallas_call(body, name='relay', out_shape=(jax.ShapeDtypeStruct((ROWS,...  92.3 us
    pallas_call x1, Pallas kernels, shards(): pl.pallas_call(hand_out, name='hand_out', out_shape=(jax.ShapeDtypeStruct...  3.66 us

profile of v3, /device:TPU:6, one launch (start us, length us, event | category | flops | bytes accessed | tf_op | source)
XLA Modules:
  0.0 96.6 jit_solution(6153289306145628306)
XLA Ops:
  0.6 92.3 %relay.1 = (bf16[128,256]{1,0:T(8,128)(2,1)}, bf16[128,256]{1,0:T(8,128)(2,1)}, f32[16,256]{1,0:T(8,128)}, bf16[4,256,256]{2,1,0:T(8,128)(2,1)}, bf16[4,256,256]...) custom-call(bf16[128,256]{1,0:T(8,128)(2,1)} %bitcast.15, bf16[4,4,256]{2,1,0:T(4,128)(2,1)} %mem.1, f32[1,4096]{1,0:T(1,128)} %lgain.1, ...), custom_call_target="tpu_custom_call" | custom-call | tf_op jit(solution)/shard_map/relay/pallas_call | solution.py:589
  92.9 3.7 %hand_out.1 = (bf16[4,4,256]{2,1,0:T(4,128)(2,1)}, bf16[128,256]{1,0:T(8,128)(2,1)}, bf16[128,256]{1,0:T(8,128)(2,1)}, bf16[4,256,256]{2,1,0:T(8,128)(2,1)}, bf1...) custom-call(f32[16,256]{1,0:T(8,128)} %get-tuple-element.18.mg, bf16[128,256]{1,0:T(8,128)(2,1)} %get-tuple-element.19.mix, ...), custom_call_target="tpu_custom_call" | custom-call | tf_op jit(solution)/shard_map/hand_out/pallas_call | solution.py:646

commit v4 on v3

--- a/solution.py
+++ b/solution.py
@@ -42,7 +42,7 @@
 def body(
     stream, mem, lgain, fgain, wq, wk, wv, cot, enc_len, dec_len, assign,
     mix_o, sg_o, mg_o, dq_o, dk_o, dv_o,
-    piece, gat, xm, sq, wf, acc, inv, g_own, g_all, x_all, x_rel, part, rs, dots, rsd, h_out, h_in,
+    piece, gat, xm, sq, wf, acc, inv, qkv, soft, up, g_own, g_all, x_all, x_rel, part, rs, dots, rsd, h_out, h_in,
     ag_s, ag_r, wy_s, wy_r, wc_s, wc_r, wr_s, wr_r, m_s, m_r, ex_s, ex_r, rs_s, rs_r, d_s, d_r, h_s, h_r, loc,
 ):
     s = lax.axis_index("section")
@@ -99,20 +99,23 @@
             around[direction],
         )
 
-    def weight_far(w):
-        return remote(
-            wf.at[w, pl.ds(4 * d, 4)], wf.at[w, pl.ds(4 * d, 4)], wy_s.at[w], wy_r.at[w], {"dp": far}
-        )
+    def weight_part(w, quarter, owner):
+        if w < 2:
+            return wf.at[w, pl.ds(4 * owner, 4)], w
+        return wf.at[w, pl.ds(4 * owner + quarter, 1)], w + quarter
+
+    def weight_far(w, quarter=0):
+        block, at = weight_part(w, quarter, d)
+        return remote(block, block, wy_s.at[at], wy_r.at[at], {"dp": far})
 
     def weight_mate(w):
         return remote(
             wf.at[w, pl.ds(4 * d, 4)], wf.at[w, pl.ds(4 * d, 4)], wc_s.at[w], wc_r.at[w], {"dp": mate}
         )
 
-    def weight_relay(w):
-        return remote(
-            wf.at[w, pl.ds(4 * far, 4)], wf.at[w, pl.ds(4 * far, 4)], wr_s.at[w], wr_r.at[w], {"dp": mate}
-        )
+    def weight_relay(w, quarter=0):
+        block, at = weight_part(w, quarter, far)
+        return remote(block, block, wr_s.at[at], wr_r.at[at], {"dp": mate})
 
     def mem_send(i):
         return remote(
@@ -136,7 +139,8 @@
         ring(0, way, 1).start()
     for w in range(3):
         own[1 + w].wait()
-        weight_far(w).start()
+        for quarter in range(4 if w == 2 else 1):
+            weight_far(w, quarter).start()
 
     for w in range(3):
         weight_mate(w).start()
@@ -280,10 +284,7 @@
 
         acc[w] = lax.fori_loop(0, half, step, acc[w])
 
-    for w in range(3):
-        if w == 2:
-            weight_far(2).wait_recv()
-            weight_relay(2).start()
+    for w in range(2):
         weight_relay(w).wait_recv()
         project(w)
 
@@ -310,25 +311,94 @@
 
     q_scale = jnp.concatenate([inv[0], inv[0]], axis=1)
     s_scale = jnp.concatenate([inv[1], inv[1]], axis=1)
-    queries = (acc[0] * q_scale).astype(BF16)
-    keys = (acc[1] * s_scale).astype(BF16)
-    values = (acc[2] * s_scale).astype(BF16)
+    qkv[0] = (acc[0] * q_scale).astype(BF16)
+    qkv[1] = (acc[1] * s_scale).astype(BF16)
     scale = HEAD_DIM**-0.5
     for h in range(WIDE // HEAD_DIM):
         at = slice(h * HEAD_DIM, (h + 1) * HEAD_DIM)
-        qh, kh, vh = queries[:, at], keys[:, at], values[:, at]
-        scores = jnp.where(live, dot_nt(qh, kh) * scale, -1e30)
+        scores = jnp.where(live, dot_nt(qkv[0, :, at], qkv[1, :, at]) * scale, -1e30)
         raised = jnp.exp(scores - jnp.max(scores, axis=1, keepdims=True))
-        weights = raised / jnp.sum(raised, axis=1, keepdims=True)
+        soft[h] = raised / jnp.sum(raised, axis=1, keepdims=True)
+        up[:, at] = (cot[:, at].astype(F32) * row_live).astype(BF16)
+
+    def add_values(i):
+        acc[2] = acc[2] + dot_nn(xm[src, i], wf[2, i])
+
+    for quarter in range(4):
+        weight_far(2, quarter).wait_recv()
+        weight_relay(2, quarter).start()
+        add_values(4 * far + quarter)
+        if quarter > 0:
+            weight_relay(2, quarter - 1).wait_recv()
+            add_values(4 * far_mate + quarter - 1)
+    weight_relay(2, 3).wait_recv()
+    add_values(4 * far_mate + 3)
+    qkv[2] = (acc[2] * jnp.concatenate([inv[1], inv[1]], axis=1)).astype(BF16)
+
+    for h in range(WIDE // HEAD_DIM):
+        at = slice(h * HEAD_DIM, (h + 1) * HEAD_DIM)
+        qh, kh, vh, upstream = qkv[0, :, at], qkv[1, :, at], qkv[2, :, at], up[:, at]
+        weights = soft[h]
         probs = weights.astype(BF16)
         mix_o[:, at] = (dot_nn(probs, vh) * row_live).astype(BF16)
-        upstream = (cot[:, at].astype(F32) * row_live).astype(BF16)
         grad_weights = dot_nt(upstream, vh)
         inner = jnp.sum(grad_weights * weights, axis=1, keepdims=True)
         grad_scores = (weights * (grad_weights - inner) * scale).astype(BF16)
         g_own[0, :, at] = (dot_nn(grad_scores, kh) * inv[0][:, 0:HEAD_DIM]).astype(BF16)
         g_own[1, :, at] = (dot_tn(grad_scores, qh) * inv[1][:, 0:HEAD_DIM]).astype(BF16)
         g_own[2, :, at] = (dot_tn(probs, upstream) * inv[1][:, 0:HEAD_DIM]).astype(BF16)
+
+    def back(i):
+        grad_q = dot_nt(g_own[0], wf[0, i])
+        grad_s = dot_nt(g_own[1], wf[1, i]) + dot_nt(g_own[2], wf[2, i])
+        part[0, i] = jnp.where(is_dec, grad_q, grad_q + grad_s).astype(BF16)
+        part[1, i] = grad_s.astype(BF16)
+
+    def chain_at(way_hops, direction, k):
+        ahead = way_hops + 1 - k
+        return lax.rem(z + ahead, N_TP) if direction == 0 else lax.rem(z - ahead + N_TP, N_TP)
+
+    def chain(side, way, k, first):
+        direction, chunk = way
+        rows = pl.ds(chunk * HALF, HALF)
+        begin = (
+            part.at[side, chain_at(hops(way), direction, k), rows] if first else rs.at[side, direction, k - 2, rows]
+        )
+        return remote(
+            begin, rs.at[side, direction, k - 1, rows],
+            rs_s.at[side, direction, chunk, k - 1], rs_r.at[side, direction, chunk, k - 1], around[direction],
+        )
+
+    def chain_dots(direction, k, first):
+        begin = dots if first else rsd.at[direction, k - 2]
+        return remote(begin, rsd.at[direction, k - 1], d_s.at[direction, k - 1], d_r.at[direction, k - 1], around[direction])
+
+    def chain_first(way):
+        pl.when(is_dec)(lambda: chain(1, way, 1, True).start())
+        chain(0, way, 1, True).start()
+
+    back(lax.rem(z + half, N_TP))
+    chain_first((0, 0))
+    chain_first((1, 1))
+    back(lax.rem(z + half - 1, N_TP))
+    chain_first((0, 1))
+    back(lax.rem(z + half + 1, N_TP))
+    chain_first((1, 0))
+
+    def g_far():
+        return remote(g_own, g_all.at[:, d], ex_s.at[2, 0], ex_r.at[2, 0], {"dp": far})
+
+    def g_mate():
+        return remote(g_own, g_all.at[:, d], ex_s.at[2, 2], ex_r.at[2, 2], {"dp": mate})
+
+    def g_relay():
+        return remote(g_all.at[:, far], g_all.at[:, far], ex_s.at[2, 3], ex_r.at[2, 3], {"dp": mate})
+
+    g_keep = pltpu.make_async_copy(g_own, g_all.at[:, d], loc.at[6])
+    g_far().start()
+    g_mate().start()
+    g_keep.start()
+    pl.when(is_dec)(lambda: start_exchange(1))
 
     shared_dot = g_own[1].astype(F32) * acc[1] + g_own[2].astype(F32) * acc[2]
     query_dot = g_own[0].astype(F32) * acc[0]
@@ -337,62 +407,8 @@
         column = jnp.sum(total, axis=1, keepdims=True) * (1.0 / (N_TP * WIDE)) * inv[side] * inv[side]
         across = jnp.sum(jnp.where(diagonal, column, 0.0), axis=0, keepdims=True)
         dots[:, side * 128 : (side + 1) * 128] = jnp.broadcast_to(across, (8, 128))
-
-    def back(i):
-        grad_q = dot_nt(g_own[0], wf[0, i])
-        grad_s = dot_nt(g_own[1], wf[1, i]) + dot_nt(g_own[2], wf[2, i])
-        part[0, i] = jnp.where(is_dec, grad_q, grad_q + grad_s).astype(BF16)
-        part[1, i] = grad_s.astype(BF16)
-
-    def chain_at(way_hops, direction, k):
-        ahead = way_hops + 1 - k
-        return lax.rem(z + ahead, N_TP) if direction == 0 else lax.rem(z - ahead + N_TP, N_TP)
-
-    def chain(side, way, k, first):
-        direction, chunk = way
-        rows = pl.ds(chunk * HALF, HALF)
-        begin = (
-            part.at[side, chain_at(hops(way), direction, k), rows] if first else rs.at[side, direction, k - 2, rows]
-        )
-        return remote(
-            begin, rs.at[side, direction, k - 1, rows],
-            rs_s.at[side, direction, chunk, k - 1], rs_r.at[side, direction, chunk, k - 1], around[direction],
-        )
-
-    def chain_dots(direction, k, first):
-        begin = dots if first else rsd.at[direction, k - 2]
-        return remote(begin, rsd.at[direction, k - 1], d_s.at[direction, k - 1], d_r.at[direction, k - 1], around[direction])
-
-    back(lax.rem(z + half, N_TP))
-    back(lax.rem(z + half - 1, N_TP))
-    back(lax.rem(z + half + 1, N_TP))
-
-    def chain_first(side):
-        for way in WAYS:
-            chain(side, way, 1, True).start()
-
-    @pl.when(is_dec)
-    def _():
-        chain_first(1)
-
-    chain_first(0)
     chain_dots(0, 1, True).start()
     chain_dots(1, 1, True).start()
-
-    def g_far():
-        return remote(g_own, g_all.at[:, d], ex_s.at[2, 0], ex_r.at[2, 0], {"dp": far})
-
-    def g_mate():
-        return remote(g_own, g_all.at[:, d], ex_s.at[2, 2], ex_r.at[2, 2], {"dp": mate})
-
-    def g_relay():
-        return remote(g_all.at[:, far], g_all.at[:, far], ex_s.at[2, 3], ex_r.at[2, 3], {"dp": mate})
-
-    g_keep = pltpu.make_async_copy(g_own, g_all.at[:, d], loc.at[6])
-    g_far().start()
-    g_mate().start()
-    g_keep.start()
-    pl.when(is_dec)(lambda: start_exchange(1))
 
     def chain_step(k, _):
         back(lax.rem(z + half - k, N_TP))
@@ -524,9 +540,10 @@
     drain(0)
     pl.when(is_dec)(lambda: drain(1))
     for w in range(3):
-        weight_far(w).wait_send()
         weight_mate(w).wait_send()
-        weight_relay(w).wait_send()
+        for quarter in range(4 if w == 2 else 1):
+            weight_far(w, quarter).wait_send()
+            weight_relay(w, quarter).wait_send()
     for i in range(N_SECTION - FIRST_DECODER):
         @pl.when(s != FIRST_DECODER + i)
         def _():
@@ -558,24 +575,14 @@
                 give_memory(i).wait_send()
 
 
-def hand_out(mg, mix, sg, dq, dk, dv, mg_o, mix_o, sg_o, dq_o, dk_o, dv_o, small, large, sem):
-    places = (small.at[0], small.at[1], large.at[0], large.at[1], large.at[2])
-    taken = [
-        pltpu.make_async_copy(a, b, sem.at[0, n]) for n, (a, b) in enumerate(zip((mix, sg, dq, dk, dv), places))
-    ]
-    given = [
-        pltpu.make_async_copy(a, b, sem.at[1, n])
-        for n, (a, b) in enumerate(zip(places, (mix_o, sg_o, dq_o, dk_o, dv_o)))
-    ]
-    for c in taken:
-        c.start()
+def hand_out(mix, sg, mg, dq, dk, dv, mix_o, sg_o, mg_o, dq_o, dk_o, dv_o):
+    mix_o[...] = mix[...]
+    sg_o[...] = sg[...]
     for n in range(4):
         mg_o[n] = mg[n * 4 : n * 4 + 4].astype(BF16)
-    for a, b in zip(taken, given):
-        a.wait()
-        b.start()
-    for c in given:
-        c.wait()
+    dq_o[...] = dq[...]
+    dk_o[...] = dk[...]
+    dv_o[...] = dv[...]
 
 
 def shards(
@@ -608,6 +615,9 @@
             pltpu.VMEM((3, ROWS, WIDE), F32),
             pltpu.VMEM((2, ROWS, 128), F32),
             pltpu.VMEM((3, ROWS, WIDE), BF16),
+            pltpu.VMEM((4, ROWS, ROWS), F32),
+            pltpu.VMEM((ROWS, WIDE), BF16),
+            pltpu.VMEM((3, ROWS, WIDE), BF16),
             pltpu.VMEM((3, N_DP, ROWS, WIDE), BF16),
             pltpu.VMEM((2, 4, N_DP, ROWS, WIDE), BF16),
             pltpu.VMEM((2, 4, ROWS, WIDE), BF16),
@@ -618,7 +628,7 @@
             pltpu.VMEM((N_SECTION, PIECE, WIDE), F32),
             pltpu.VMEM((N_SECTION - FIRST_DECODER, PIECE, WIDE), F32),
             dma((2, 2, 2, 8)), dma((2, 2, 2, 8)),
-            dma((3,)), dma((3,)), dma((3,)), dma((3,)), dma((3,)), dma((3,)),
+            dma((6,)), dma((6,)), dma((3,)), dma((3,)), dma((6,)), dma((6,)),
             dma((4,)), dma((1,)),
             dma((3, 4)), dma((3, 4)),
             dma((2, 2, 2, 8)), dma((2, 2, 2, 8)),
@@ -642,26 +652,20 @@
         decoder_lengths,
         assignment.reshape(4),
     )
-    mixture, stream_grad, memory_grad, dq, dk, dv = outs
-    memory_grad, mixture, stream_grad, dq, dk, dv = pl.pallas_call(
+    mixture, stream_grad, memory_grad, dq, dk, dv = pl.pallas_call(
         hand_out,
         name="hand_out",
         out_shape=(
-            jax.ShapeDtypeStruct((4, 4, WIDE), BF16),
             jax.ShapeDtypeStruct((ROWS, WIDE), BF16),
             jax.ShapeDtypeStruct((ROWS, WIDE), BF16),
+            jax.ShapeDtypeStruct((4, 4, WIDE), BF16),
             jax.ShapeDtypeStruct((4, WIDE, WIDE), BF16),
             jax.ShapeDtypeStruct((4, WIDE, WIDE), BF16),
             jax.ShapeDtypeStruct((4, WIDE, WIDE), BF16),
         ),
-        in_specs=[vmem] + [hbm] * 5,
-        out_specs=(vmem,) + (hbm,) * 5,
-        scratch_shapes=[
-            pltpu.VMEM((2, ROWS, WIDE), BF16),
-            pltpu.VMEM((3, 4, WIDE, WIDE), BF16),
-            dma((2, 5)),
-        ],
-    )(memory_grad, mixture, stream_grad, dq, dk, dv)
+        in_specs=[vmem] * 6,
+        out_specs=(vmem,) * 6,
+    )(*outs)
     rows = (1, 4, 32, WIDE)
     square = (1, 4 * WIDE, WIDE)
     return (

time: 98.4 us -> 96.5 us (0.981)
  Pallas kernels: 95.9 us -> 94.9 us
    pallas_call x1, Pallas kernels: 3.66 us -> 2.64 us  [shards(): pl.pallas_call(hand_out, name='hand_out', out_shape=(jax.ShapeDtypeStruct...]
where the time goes in v4:
time: 96.5 us; the launch traced here: 95.6 us
  Pallas kernels  94.9 us (98%)
    pallas_call x1, Pallas kernels, shards(): pl.pallas_call(body, name='relay', out_shape=(jax.ShapeDtypeStruct((ROWS,...  92.3 us
    pallas_call x1, Pallas kernels, shards(): pl.pallas_call(hand_out, name='hand_out', out_shape=(jax.ShapeDtypeStruct...  2.64 us

profile of v4, /device:TPU:6, one launch (start us, length us, event | category | flops | bytes accessed | tf_op | source)
XLA Modules:
  0.0 95.6 jit_solution(2919035023404361534)
XLA Ops:
  0.6 92.3 %relay.1 = (bf16[128,256]{1,0:T(8,128)(2,1)}, bf16[128,256]{1,0:T(8,128)(2,1)}, f32[16,256]{1,0:T(8,128)}, bf16[4,256,256]{2,1,0:T(8,128)(2,1)}, bf16[4,256,256]...) custom-call(bf16[128,256]{1,0:T(8,128)(2,1)} %bitcast.15, bf16[4,4,256]{2,1,0:T(4,128)(2,1)} %mem.1, f32[1,4096]{1,0:T(1,128)} %lgain.1, ...), custom_call_target="tpu_custom_call" | custom-call | tf_op jit(solution)/shard_map/relay/pallas_call | solution.py:596
  92.9 2.6 %hand_out.1 = (bf16[128,256]{1,0:T(8,128)(2,1)}, bf16[128,256]{1,0:T(8,128)(2,1)}, bf16[4,4,256]{2,1,0:T(4,128)(2,1)}, bf16[4,256,256]{2,1,0:T(8,128)(2,1)}, bf1...) custom-call(bf16[128,256]{1,0:T(8,128)(2,1)} %get-tuple-element.18.mix, bf16[128,256]{1,0:T(8,128)(2,1)} %get-tuple-element.19.sg, ...), custom_call_target="tpu_custom_call" | custom-call | tf_op jit(solution)/shard_map/hand_out/pallas_call | solution.py:655

commit v5 on v4

--- a/solution.py
+++ b/solution.py
@@ -17,10 +17,11 @@
 N_DP = 4
 ROWS = 128
 WIDE = 256
-HALF = 64
+CHUNKS = 4
+HALF = ROWS // CHUNKS
 PIECE = 16
 FIRST_DECODER = N_SECTION // 2
-WAYS = [(0, 0), (1, 0), (0, 1), (1, 1)]
+WAYS = [(direction, chunk) for chunk in range(CHUNKS) for direction in range(2)]
 
 
 def dot_nn(a, b):
@@ -36,7 +37,7 @@
 
 
 def hops(way):
-    return N_TP // 2 if way[0] == way[1] else N_TP // 2 - 1
+    return N_TP // 2 if way[0] == way[1] % 2 else N_TP // 2 - 1
 
 
 def body(
@@ -373,17 +374,19 @@
         begin = dots if first else rsd.at[direction, k - 2]
         return remote(begin, rsd.at[direction, k - 1], d_s.at[direction, k - 1], d_r.at[direction, k - 1], around[direction])
 
-    def chain_first(way):
-        pl.when(is_dec)(lambda: chain(1, way, 1, True).start())
-        chain(0, way, 1, True).start()
+    def chain_first(direction, long):
+        for way in WAYS:
+            if way[0] == direction and (hops(way) == half) == long:
+                pl.when(is_dec)(lambda: chain(1, way, 1, True).start())
+                chain(0, way, 1, True).start()
 
     back(lax.rem(z + half, N_TP))
-    chain_first((0, 0))
-    chain_first((1, 1))
+    chain_first(0, True)
+    chain_first(1, True)
     back(lax.rem(z + half - 1, N_TP))
-    chain_first((0, 1))
+    chain_first(0, False)
     back(lax.rem(z + half + 1, N_TP))
-    chain_first((1, 0))
+    chain_first(1, False)
 
     def g_far():
         return remote(g_own, g_all.at[:, d], ex_s.at[2, 0], ex_r.at[2, 0], {"dp": far})
@@ -503,10 +506,11 @@
     def _():
         gain = fgain[0:1, here]
         column = column_of(1)
-        for chunk in range(2):
+        for chunk in range(CHUNKS):
             rows = slice(chunk * HALF, (chunk + 1) * HALF)
             value = gain * arrived(1, chunk) - gat[1, z, rows].astype(F32) * column[rows]
-            h_out[chunk * 4 : chunk * 4 + 4] = value.reshape(4, PIECE, WIDE)
+            count = HALF // PIECE
+            h_out[chunk * count : chunk * count + count] = value.reshape(count, PIECE, WIDE)
         for i in range(N_SECTION):
             @pl.when(s != i)
             def _():
@@ -515,7 +519,7 @@
 
     gain_here = lgain[0:1, here]
     stream_column = column_of(0)
-    for chunk in range(2):
+    for chunk in range(CHUNKS):
         rows = slice(chunk * HALF, (chunk + 1) * HALF)
         value = gain_here * arrived(0, chunk) - stream[rows].astype(F32) * stream_column[rows]
         sg_o[rows] = value.astype(BF16)
@@ -627,11 +631,11 @@
             pltpu.VMEM((2, N_TP // 2, 8, 256), F32),
             pltpu.VMEM((N_SECTION, PIECE, WIDE), F32),
             pltpu.VMEM((N_SECTION - FIRST_DECODER, PIECE, WIDE), F32),
-            dma((2, 2, 2, 8)), dma((2, 2, 2, 8)),
+            dma((2, 2, CHUNKS, 8)), dma((2, 2, CHUNKS, 8)),
             dma((6,)), dma((6,)), dma((3,)), dma((3,)), dma((6,)), dma((6,)),
             dma((4,)), dma((1,)),
             dma((3, 4)), dma((3, 4)),
-            dma((2, 2, 2, 8)), dma((2, 2, 2, 8)),
+            dma((2, 2, CHUNKS, 8)), dma((2, 2, CHUNKS, 8)),
             dma((2, 8)), dma((2, 8)),
             dma((8,)), dma((1,)),
             dma((7,)),

time: 96.5 us -> 98.1 us (1.017)
  Pallas kernels: 94.9 us -> 96.3 us
    pallas_call x1, Pallas kernels: 92.3 us -> 93.7 us  [shards(): pl.pallas_call(body, name='relay', out_shape=(jax.ShapeDtypeStruct((ROWS,...]
where the time goes in v5:
time: 98.1 us; the launch traced here: 97 us
  Pallas kernels  96.3 us (98%)
    pallas_call x1, Pallas kernels, shards(): pl.pallas_call(body, name='relay', out_shape=(jax.ShapeDtypeStruct((ROWS,...  93.7 us
    pallas_call x1, Pallas kernels, shards(): pl.pallas_call(hand_out, name='hand_out', out_shape=(jax.ShapeDtypeStruct...  2.64 us

profile of v5, /device:TPU:6, one launch (start us, length us, event | category | flops | bytes accessed | tf_op | source)
XLA Modules:
  0.0 97.0 jit_solution(212309589951800954)
XLA Ops:
  0.6 93.7 %relay.1 = (bf16[128,256]{1,0:T(8,128)(2,1)}, bf16[128,256]{1,0:T(8,128)(2,1)}, f32[16,256]{1,0:T(8,128)}, bf16[4,256,256]{2,1,0:T(8,128)(2,1)}, bf16[4,256,256]...) custom-call(bf16[128,256]{1,0:T(8,128)(2,1)} %bitcast.15, bf16[4,4,256]{2,1,0:T(4,128)(2,1)} %mem.1, f32[1,4096]{1,0:T(1,128)} %lgain.1, ...), custom_call_target="tpu_custom_call" | custom-call | tf_op jit(solution)/shard_map/relay/pallas_call | solution.py:600
  94.3 2.6 %hand_out.1 = (bf16[128,256]{1,0:T(8,128)(2,1)}, bf16[128,256]{1,0:T(8,128)(2,1)}, bf16[4,4,256]{2,1,0:T(4,128)(2,1)}, bf16[4,256,256]{2,1,0:T(8,128)(2,1)}, bf1...) custom-call(bf16[128,256]{1,0:T(8,128)(2,1)} %get-tuple-element.18.mix, bf16[128,256]{1,0:T(8,128)(2,1)} %get-tuple-element.19.sg, ...), custom_call_target="tpu_custom_call" | custom-call | tf_op jit(solution)/shard_map/hand_out/pallas_call | solution.py:659
